TPU v7x, 512 devices: a whole 4x8x8 slice. The times are simulated.
512 devices in a mesh: dp: 128 (over z, y, core), shard: 4 (over x).
Axes of the slice: x: 4, y: 8, z: 8, core: 2. Of those that a mesh axis runs over, the one named last changes fastest.
Arguments:
- latent_grads: bfloat16 [128, 288, 2560], P('dp', None, 'shard'), may hold values from -132 to 132
- latent_errors: bfloat16 [128, 288, 2560], P('dp', None, 'shard'), may hold values from -3 to 3
- latent_moments: bfloat16 [288, 2560], P(None, 'shard'), may hold values from -2 to 2
- latent_coeffs: bfloat16 [2560, 32], P('shard'), may hold values from -5 to 5
- expand_grads: bfloat16 [128, 5120, 256], P('dp', 'shard'), may hold values from -132 to 132
- expand_errors: bfloat16 [128, 5120, 256], P('dp', 'shard'), may hold values from -3 to 3
- expand_moments: bfloat16 [5120, 256], P('shard'), may hold values from -2 to 2
- expand_coeffs: bfloat16 [256, 32], replicated, may hold values from -5 to 5
- gain_grads: bfloat16 [128, 256], P('dp'), may hold values from -132 to 132
- gain_moments: float32 [256], P('shard'), may hold values from -5 to 5
Outputs:
- latent_leftover: bfloat16 [128, 288, 2560], P('dp', None, 'shard')
- latent_momentum: bfloat16 [288, 2560], P(None, 'shard')
- latent_factor: bfloat16 [2560, 32], P('shard')
- expand_leftover: bfloat16 [128, 5120, 256], P('dp', 'shard')
- expand_momentum: bfloat16 [5120, 256], P('shard')
- expand_factor: bfloat16 [256, 32], replicated
- gain_momentum: float32 [256], P('shard')
All inputs are finite; a program needn't handle non-finite values.
Results may differ from a plain program's by a relative error of at most 0.0044.
The roundings to bfloat16 on the way count: a program that leaves them out, or rounds other values in their place, can miss the bound.
Values may be sent and summed in bfloat16 or wider, within the bound.
No kernel may reach another device: no remote copies, remote signals or barrier semaphores. Data moves between devices by JAX's collectives and lax.ppermute only.
A program may use at most 64 MiB of HBM per device.

v0:
```python
import jax
import jax.numpy as jnp
from jax import lax
from jax.sharding import PartitionSpec as P

NS_ITERS = 6


BETA = 0.9
EPSILON = 1e-06
HIGHEST = lax.Precision.HIGHEST


def inverse_root(gram_matrix):
    trace_sum = jnp.trace(gram_matrix) + EPSILON
    identity = jnp.eye(gram_matrix.shape[0], dtype=jnp.float32)
    root_left = gram_matrix / trace_sum
    root_right = identity
    for repeat_index in range(NS_ITERS):
        middle = 1.5 * identity - 0.5 * jnp.dot(root_right, root_left, precision=HIGHEST)
        root_left = jnp.dot(root_left, middle, precision=HIGHEST)
        root_right = jnp.dot(middle, root_right, precision=HIGHEST)
    return root_right / jnp.sqrt(trace_sum)


def self_gram(matrix):
    return jnp.dot(matrix.T, matrix, precision=HIGHEST)


def finish(combined, basis_rows, right_sum, moments, replicas):
    factor = (right_sum / replicas).astype(jnp.bfloat16)
    approx = jnp.einsum("nr,mr->nm", basis_rows, factor, preferred_element_type=jnp.float32)
    leftover = (combined - approx).astype(jnp.bfloat16)[None]
    momentum = (BETA * moments.astype(jnp.float32) + approx).astype(jnp.bfloat16)
    return (leftover, momentum, factor)


def local(
    latent_grads,
    latent_errors,
    latent_moments,
    latent_coeffs,
    expand_grads,
    expand_errors,
    expand_moments,
    expand_coeffs,
    gain_grads,
    gain_moments,
):
    replicas = lax.axis_size("dp")
    latent_total = latent_grads[0].astype(jnp.float32) + latent_errors[0].astype(jnp.float32)
    latent_merged = latent_total.astype(jnp.bfloat16)
    expand_total = expand_grads[0].astype(jnp.float32) + expand_errors[0].astype(jnp.float32)
    expand_merged = expand_total.astype(jnp.bfloat16)
    latent_part = jnp.dot(latent_merged, latent_coeffs, preferred_element_type=jnp.float32)
    expand_part = jnp.dot(expand_merged, expand_coeffs, preferred_element_type=jnp.float32)
    owned_width = gain_moments.shape[0]
    offset = lax.axis_index("shard") * owned_width
    gain_vector = gain_grads[0].astype(jnp.float32)
    latent_summed = lax.psum(latent_part, ("dp", "shard"))
    gain_summed = lax.psum(gain_vector, "dp")
    expand_summed = lax.psum(expand_part, "dp")
    gain_summed = lax.dynamic_slice_in_dim(gain_summed, offset, owned_width)
    gain_momentum = BETA * gain_moments + gain_summed / replicas
    latent_basis = jnp.dot(
        latent_summed, inverse_root(self_gram(latent_summed)), precision=HIGHEST
    ).astype(jnp.bfloat16)
    expand_gram = lax.psum(self_gram(expand_summed), "shard")
    expand_basis = jnp.dot(expand_summed, inverse_root(expand_gram), precision=HIGHEST).astype(
        jnp.bfloat16
    )
    latent_qpart = jnp.einsum(
        "nm,nr->mr", latent_merged, latent_basis, preferred_element_type=jnp.float32
    )
    expand_qpart = jnp.einsum(
        "nm,nr->mr", expand_merged, expand_basis, preferred_element_type=jnp.float32
    )
    latent_right = lax.psum(latent_qpart, "dp")
    expand_right = lax.psum(expand_qpart, ("dp", "shard"))
    latent_leftover, latent_momentum, latent_factor = finish(
        latent_total, latent_basis, latent_right, latent_moments, replicas
    )
    expand_leftover, expand_momentum, expand_factor = finish(
        expand_total, expand_basis, expand_right, expand_moments, replicas
    )
    return (
        latent_leftover,
        latent_momentum,
        latent_factor,
        expand_leftover,
        expand_momentum,
        expand_factor,
        gain_momentum,
    )


def solution(mesh):
    return jax.shard_map(
        local,
        mesh=mesh,
        in_specs=(
            P("dp", None, "shard"),
            P("dp", None, "shard"),
            P(None, "shard"),
            P("shard", None),
            P("dp", "shard", None),
            P("dp", "shard", None),
            P("shard", None),
            P(),
            P("dp", None),
            P("shard"),
        ),
        out_specs=(
            P("dp", None, "shard"),
            P(None, "shard"),
            P("shard", None),
            P("dp", "shard", None),
            P("shard", None),
            P(),
            P("shard"),
        ),
        check_vma=False,
    )
```

profile of v0, /device:TPU:1, one launch (start us, length us, event | category | flops | bytes accessed | tf_op | source)
XLA Modules:
  0.0 730.6 jit_solution(8128142761487943919)
XLA Ops:
  7.2 2.4 fusion.17
  9.7 0.9 fusion.19
  10.6 254.7 %psum.47 = f32[256]{0:T(256)S(1)} all-reduce(f32[256]{0:T(256)S(1)} %bitcast.99), channel_id=1, replica_groups=mesh['dp'=128,'shard'=4] {'dp'}, use_global_device_ids=true, to_apply=%region_7.8 | all-reduce | flops 256 | bytes 2048 | tf_op jit(solution)/shard_map/psum | solution.py:61
  265.3 1.3 fusion.32
  266.7 13.3 %psum.45 = f32[32,32]{1,0:T(8,128)S(1)} all-reduce(f32[32,32]{1,0:T(8,128)S(1)} %fusion.32), channel_id=1, replica_groups=mesh['dp'=128,'shard'=4] {'shard'}, use_global_device_ids=true, to_apply=%region_4.5 | all-reduce | flops 1024 | bytes 8192 | tf_op jit(solution)/shard_map/psum | solution.py:68
  279.9 0.6 select_reduce_fusion
  281.3 0.1 fusion.23
  281.5 0.1 fusion.20
  281.6 0.2 fusion.5
  281.8 0.1 fusion.34
  281.9 0.1 fusion.33
  282.1 0.2 fusion.4
  282.2 0.1 fusion.36
  282.4 0.1 fusion.35
  282.5 0.2 fusion.3
  282.7 0.1 fusion.38
  282.8 0.1 fusion.37
  283.0 0.2 fusion.2
  283.1 0.1 fusion.40
  283.3 0.1 fusion.39
  283.5 0.1 fusion.1
  283.7 0.1 convolution_divide_fusion
  283.8 0.3 convolution_convert_fusion
  284.2 0.9 fusion.16
  285.2 0.6 multiply_add_fusion
  285.8 256.9 %all-reduce.9.cloned.1.call-done = (f32[288,32]{0,1:T(8,128)}, f32[256,32]{0,1:T(8,128)}) async-done(((f32[288,32]{0,1:T(8,128)}, f32[256,32]{0,1:T(8,128)}), (f32[288,32]{0,1:T(8,128)}, f32[256,32]{0,1:T(8,128)})) %all-reduce.9.cloned.1.call-update) | async-done | bytes 69648 | tf_op jit(solution)/shard_map/psum | solution.py:60
  542.7 1.7 select_reduce_fusion.1
  545.2 0.1 fusion.22
  545.3 0.1 fusion.21
  545.4 0.2 fusion.11
  545.6 0.1 fusion.25
  545.7 0.1 fusion.24
  545.9 0.2 fusion.10
  546.1 0.1 fusion.27
  546.2 0.1 fusion.26
  546.4 0.2 fusion.9
  546.5 0.1 fusion.29
  546.7 0.1 fusion.28
  546.8 0.1 fusion.8
  547.0 0.1 fusion.31
  547.1 0.1 fusion.30
  547.5 0.1 convolution_divide_fusion.1
  547.7 0.2 convolution_convert_fusion.1
  547.9 0.9 fusion.18
  548.8 1.6 add_convert_fusion
  550.4 171.6 %all-reduce.5.cloned.1.call-done = f32[640,32]{0,1:T(8,128)} async-done(((f32[640,32]{0,1:T(8,128)}), f32[640,32]{0,1:T(8,128)}) %all-reduce.5.cloned.1.call-update) | async-done | bytes 81936 | tf_op jit(solution)/shard_map/psum | solution.py:78
  722.0 0.9 multiply_convert_fusion
  722.9 1.2 add_convert_fusion.1
  (40 shorter events, 0.7 us)
Async XLA Ops:
  7.2 2.5 copy-start
  7.2 2.5 copy-start.4
  7.2 2.5 copy-start.3
  7.2 258.1 %all-reduce.7.cloned.1.call-start = ((), (), s32[]{:S(2)}) async-start(), calls=%async_computation.1 | async-start | bytes 327680 | tf_op jit(solution)/shard_map/psum | solution.py:62
  9.6 1.0 copy-start.12
  9.6 533.0 %all-reduce.9.cloned.1.call-start = ((), (), s32[]{:S(2)}) async-start(), calls=%async_computation.2 | async-start | bytes 163840 | tf_op jit(solution)/shard_map/psum | solution.py:60
  265.3 18.5 %copy-start.5 = (f32[1280,32]{0,1:T(8,128)S(1)}, f32[1280,32]{0,1:T(8,128)}, u32[]{:S(2)}) copy-start(f32[1280,32]{0,1:T(8,128)} %all-reduce.7.cloned.1.call-done) | copy-start | bytes 491524
  265.3 18.9 %copy-start.2 = (bf16[1,1280,256]{2,1,0:T(8,128)(2,1)S(1)}, bf16[1,1280,256]{2,1,0:T(8,128)(2,1)}, u32[]{:S(2)}) copy-start(bf16[1,1280,256]{2,1,0:T(8,128)(2,1)} %param.14) | copy-start | bytes 1966084
  266.6 17.5 %copy-start.1 = (bf16[1,1280,256]{2,1,0:T(8,128)(2,1)S(1)}, bf16[1,1280,256]{2,1,0:T(8,128)(2,1)}, u32[]{:S(2)}) copy-start(bf16[1,1280,256]{2,1,0:T(8,128)(2,1)} %param.15) | copy-start | bytes 1966084
  284.2 1.0 copy-start.13
  285.1 436.9 %all-reduce.5.cloned.1.call-start = ((), (), s32[]{:S(2)}) async-start(), calls=%async_computation | async-start | bytes 163840 | tf_op jit(solution)/shard_map/psum | solution.py:78
  542.7 4.7 copy-start.11
  542.7 5.0 copy-start.7
  546.8 2.0 copy-start.6
  547.4 3.0 copy-start.10
  548.8 174.1 %copy-start.8 = (bf16[288,640]{1,0:T(8,128)(2,1)S(1)}, bf16[288,640]{1,0:T(8,128)(2,1)}, u32[]{:S(2)}) copy-start(bf16[288,640]{1,0:T(8,128)(2,1)} %param.12) | copy-start | bytes 1105924
  722.9 1.2 copy-start.9
Sparse Core Ops, SparseCore 0:
  11.9 191.8 all-reduce.6
  285.3 257.3 all-reduce.8
  548.9 173.0 all-reduce.4
where the time goes:
time: 731 us
  waiting for transfers between devices  429 us (59%)
  blocking collectives  268 us (37%)
  matrix products  16.3 us (2%)
  between operations  15.5 us (2%)
    psum x1, waiting for transfers between devices, local(): latent_summed = lax.psum(latent_part, ('dp', 'shard'))  257 us
    psum x1, blocking collectives, local(): gain_summed = lax.psum(gain_vector, 'dp')  255 us
    psum x1, waiting for transfers between devices, local(): latent_right = lax.psum(latent_qpart, 'dp')  172 us
  transfers between devices with their start and end apart: 3, of which 2 were waited for; matrix products, arithmetic and copies ran while one was open for 0% of the time, Pallas kernels for 0%

commit v1 on v0

v1 whole, which is shorter than its diff:
```python
import jax
import jax.numpy as jnp
from jax import lax
from jax.sharding import Mesh, PartitionSpec as P

NS_ITERS = 6
BETA = 0.9
EPSILON = 1e-06
HIGHEST = lax.Precision.HIGHEST
RANK = 32
RING = ("y", "core")
CROSS = ("z", "x")
DP = ("z", "y", "core")


def inverse_roots(grams):
    identity = jnp.eye(RANK, dtype=jnp.float32)
    trace_sum = jnp.sum(grams * identity, axis=(1, 2), keepdims=True) + EPSILON
    root_left = grams / trace_sum
    root_right = jnp.broadcast_to(identity, grams.shape)
    for repeat_index in range(NS_ITERS):
        middle = 1.5 * identity - 0.5 * jnp.matmul(root_right, root_left, precision=HIGHEST)
        root_left = jnp.matmul(root_left, middle, precision=HIGHEST)
        root_right = jnp.matmul(middle, root_right, precision=HIGHEST)
    return root_right / jnp.sqrt(trace_sum)


def spread(piece, axes, count):
    return lax.all_to_all(jnp.broadcast_to(piece, (count, *piece.shape)), axes, 0, 0)


def local(
    latent_grads,
    latent_errors,
    latent_moments,
    latent_coeffs,
    expand_grads,
    expand_errors,
    expand_moments,
    expand_coeffs,
    gain_grads,
    gain_moments,
):
    ring = lax.axis_size(RING)
    depth = lax.axis_size("z")
    shards = lax.axis_size("x")
    cross = depth * shards
    replicas = ring * depth
    shard = lax.axis_index("x")
    latent_rows, latent_cols = latent_grads.shape[1:]
    expand_rows, expand_cols = expand_grads.shape[1:]
    slab = expand_rows // ring
    latent_slabs = latent_rows // RANK
    owned = gain_moments.shape[0]
    gain_piece = owned * shards // ring

    latent_total = latent_grads[0].astype(jnp.float32) + latent_errors[0].astype(jnp.float32)
    latent_merged = latent_total.astype(jnp.bfloat16)
    expand_total = expand_grads[0].astype(jnp.float32) + expand_errors[0].astype(jnp.float32)
    expand_merged = expand_total.astype(jnp.bfloat16)

    expand_part = jnp.einsum(
        "pnk,kr->prn",
        expand_merged.reshape(ring, slab, expand_cols),
        expand_coeffs,
        preferred_element_type=jnp.float32,
    )
    latent_part = jnp.einsum(
        "pnk,kr->prn",
        latent_merged.reshape(latent_slabs, RANK, latent_cols),
        latent_coeffs,
        preferred_element_type=jnp.float32,
    )
    latent_part = jnp.pad(latent_part, ((0, ring - latent_slabs), (0, 0), (0, 0)))
    gain_part = gain_grads[0].astype(jnp.float32).reshape(ring, 1, gain_piece)
    gain_part = jnp.pad(gain_part, ((0, 0), (0, RANK - 1), (0, 0)))
    part = jnp.concatenate([expand_part, latent_part, gain_part], axis=2).astype(jnp.bfloat16)
    piece = lax.all_to_all(part, RING, 0, 0).astype(jnp.float32).sum(0)
    pieces = spread(piece.astype(jnp.bfloat16), CROSS, cross).astype(jnp.float32)
    pieces = pieces.reshape(depth, shards, RANK, -1).sum(0)
    expand_slabs = pieces[:, :, :slab]
    gram_part = jnp.einsum("xrn,xsn->rs", expand_slabs, expand_slabs, precision=HIGHEST)
    own = lax.dynamic_index_in_dim(pieces, shard, 0, keepdims=False)
    latent_slab = pieces[:, :, slab : slab + RANK].sum(0)
    mine = jnp.concatenate([own[:, :slab], latent_slab, own[:, slab + RANK :]], axis=1)
    width = mine.shape[1]
    mine = jnp.concatenate([mine, gram_part.reshape(-1, width)], axis=0)
    gathered = spread(mine, RING, ring)

    expand_left = gathered[:, :RANK, :slab]
    latent_left = gathered[:latent_slabs, :RANK, slab : slab + RANK]
    gain_summed = gathered[:, 0, slab + RANK :].reshape(-1)
    expand_gram = gathered[:, RANK:].sum(0).reshape(RANK, RANK)
    latent_gram = jnp.einsum("prn,psn->rs", latent_left, latent_left, precision=HIGHEST)
    roots = inverse_roots(jnp.stack([latent_gram, expand_gram]))
    latent_basis = jnp.einsum("prn,rs->spn", latent_left, roots[0], precision=HIGHEST)
    latent_basis = latent_basis.astype(jnp.bfloat16).reshape(RANK, latent_rows)
    expand_basis = jnp.einsum("prn,rs->spn", expand_left, roots[1], precision=HIGHEST)
    expand_basis = expand_basis.astype(jnp.bfloat16).reshape(RANK, expand_rows)

    latent_right = jnp.dot(latent_basis, latent_merged, preferred_element_type=jnp.float32)
    expand_right = jnp.dot(expand_basis, expand_merged, preferred_element_type=jnp.float32)
    right = jnp.concatenate([latent_right, expand_right], axis=1).astype(jnp.bfloat16)
    right = right.reshape(ring, RANK // ring, latent_cols + expand_cols)
    piece = lax.all_to_all(right, RING, 0, 0).astype(jnp.float32).sum(0)
    pieces = spread(piece.astype(jnp.bfloat16), CROSS, cross).astype(jnp.float32)
    pieces = pieces.reshape(depth, shards, RANK // ring, -1).sum(0)
    latent_right = lax.dynamic_index_in_dim(pieces, shard, 0, keepdims=False)[:, :latent_cols]
    expand_right = pieces[:, :, latent_cols:].sum(0)
    mine = jnp.concatenate([latent_right, expand_right], axis=1) / replicas
    factors = spread(mine.astype(jnp.bfloat16), RING, ring).reshape(RANK, -1)
    latent_factor = factors[:, :latent_cols]
    expand_factor = factors[:, latent_cols:]

    def finish(total, basis, factor, moments):
        approx = jnp.einsum("rn,rm->nm", basis, factor, preferred_element_type=jnp.float32)
        leftover = (total - approx).astype(jnp.bfloat16)[None]
        momentum = (BETA * moments.astype(jnp.float32) + approx).astype(jnp.bfloat16)
        return leftover, momentum, factor.T

    gain_summed = lax.dynamic_slice_in_dim(gain_summed, shard * owned, owned)
    gain_momentum = BETA * gain_moments + gain_summed / replicas
    return (
        *finish(latent_total, latent_basis, latent_factor, latent_moments),
        *finish(expand_total, expand_basis, expand_factor, expand_moments),
        gain_momentum,
    )


def solution(mesh):
    grid = Mesh(mesh.devices.reshape(8, 8, 2, 4), ("z", "y", "core", "x"))
    return jax.shard_map(
        local,
        mesh=grid,
        in_specs=(
            P(DP, None, "x"),
            P(DP, None, "x"),
            P(None, "x"),
            P("x", None),
            P(DP, "x", None),
            P(DP, "x", None),
            P("x", None),
            P(),
            P(DP, None),
            P("x"),
        ),
        out_specs=(
            P(DP, None, "x"),
            P(None, "x"),
            P("x", None),
            P(DP, "x", None),
            P("x", None),
            P(),
            P("x"),
        ),
        check_vma=False,
    )
```

time: 731 us -> 115 us (0.16)
  waiting for transfers between devices: 429 us -> 41.6 us
  blocking collectives: 268 us -> 28.9 us
  starting transfers between devices: 0.12 us -> 25.5 us
  between operations: 15.5 us -> 1.04 us
  matrix products: 16.3 us -> 8.11 us
    psum x3 -> x0, waiting for transfers between devices: 428 us -> none  [the longest x1 257 us: local(): latent_summed = lax.psum(latent_part, ('dp', 'shard'))]
    psum x2 -> x0, blocking collectives: 268 us -> none  [the longest x1 255 us: local(): gain_summed = lax.psum(gain_vector, 'dp')]
    all_to_all x0 -> x4, waiting for transfers between devices: none -> 41.6 us  [spread(): lax.all_to_all(jnp.broadcast_to(piece, (count, *piece.shape)), axes, 0, 0)]
    all_to_all x0 -> x2, blocking collectives: none -> 28.9 us  [the longest x1 18.5 us: local(): piece = lax.all_to_all(part, RING, 0, 0).astype(jnp.float32).sum(0)]
    all_to_all x0 -> x4, starting transfers between devices: none -> 25.5 us  [spread(): lax.all_to_all(jnp.broadcast_to(piece, (count, *piece.shape)), axes, 0, 0)]
    dot_general x44 -> x27, matrix products: 16.3 us -> 8.11 us  [the longest x2 2.69 us: finish(): jnp.einsum('rn,rm->nm', basis, factor, preferred_element_type=jnp.float32)]
  transfers between devices with their start and end apart: 3 -> 4, of which waited for: 2 -> 4; matrix products, arithmetic and copies ran while one was open for 0% -> 1% of each run, Pallas kernels for 0% -> 0%
where the time goes in v1:
time: 115 us
  waiting for transfers between devices  41.6 us (36%)
  blocking collectives  28.9 us (25%)
  starting transfers between devices  25.5 us (22%)
  matrix products  8.11 us (7%)
  local copies, waits for them, and re-layouts  5.97 us (5%)
  other arithmetic  3.47 us (3%)
    all_to_all x4, waiting for transfers between devices, spread(): lax.all_to_all(jnp.broadcast_to(piece, (count, *piece.shape)), axes, 0, 0)  41.6 us
    all_to_all x4, starting transfers between devices, spread(): lax.all_to_all(jnp.broadcast_to(piece, (count, *piece.shape)), axes, 0, 0)  25.5 us
    all_to_all x1, blocking collectives, local(): piece = lax.all_to_all(part, RING, 0, 0).astype(jnp.float32).sum(0)  18.5 us
    all_to_all x1, blocking collectives, local(): piece = lax.all_to_all(right, RING, 0, 0).astype(jnp.float32).sum(0)  10.4 us
    broadcast_in_dim x4, local copies, waits for them, and re-layouts, spread(): jnp.broadcast_to(piece, (count, *piece.shape))  2.86 us
    dot_general x2, matrix products, finish(): jnp.einsum('rn,rm->nm', basis, factor, preferred_element_type=jnp.float32)  2.69 us
  transfers between devices with their start and end apart: 4, of which 4 were waited for; matrix products, arithmetic and copies ran while one was open for 1% of the time, Pallas kernels for 0%

profile of v1, /device:TPU:1, one launch (start us, length us, event | category | flops | bytes accessed | tf_op | source)
XLA Modules:
  0.0 114.6 jit_solution(428302211725453579)
XLA Ops:
  0.6 0.7 reduce.2
  1.4 1.3 %fusion.11 = bf16[1,288,640]{2,1,0:T(8,128)(2,1)S(1)} fusion(bf16[1,288,640]{2,1,0:T(8,128)(2,1)} %param.11, bf16[1,288,640]{2,1,0:T(8,128)(2,1)} %param.10), kind=kLoop, calls=%fused_computation.32 | loop fusion | flops 737280 | bytes 1105920 | tf_op jit(solution)/shard_map/convert_element_type | solution.py:58
  2.8 0.4 fusion.3
  3.2 0.2 fusion.1
  3.4 0.5 copy-done.7
  3.9 0.4 fusion.2
  4.4 18.5 %all_to_all.30 = bf16[16,32,128]{2,1,0:T(8,128)(2,1)S(1)} all-to-all(bf16[16,32,128]{2,1,0:T(8,128)(2,1)S(1)} %fusion.23), channel_id=1, replica_groups=mesh['z'=8,'y'=8,'core'=2,'x'=4] {'y','core'}, dimensions={0} | all-to-all | bytes 262144 | tf_op jit(solution)/shard_map/all_to_all | solution.py:78
  22.9 0.7 broadcast_in_dim.34
  23.7 12.0 %all-to-all-start.1 = ((bf16[32,32,128]{2,1,0:T(8,128)(2,1)}), bf16[32,32,128]{2,1,0:T(8,128)(2,1)S(1)}, u32[]{:S(2)}, u32[]{:S(2)}) async-start(bf16[32,32,128]{2,1,0:T(8,128)(2,1)} %broadcast_in_dim.34), calls=%async_computation.1 | async-start | bytes 524288 | tf_op jit(solution)/shard_map/all_to_all | solution.py:29
  35.7 12.3 %all-to-all-done.1 = bf16[32,32,128]{2,1,0:T(8,128)(2,1)S(1)} async-done(((bf16[32,32,128]{2,1,0:T(8,128)(2,1)}), bf16[32,32,128]{2,1,0:T(8,128)(2,1)S(1)}, u32[]{:S(2)}, u32[]{:S(2)}) %all-to-all-start.1) | async-done | bytes 262176 | tf_op jit(solution)/shard_map/all_to_all | solution.py:29
  48.0 0.2 convolution_bitcast_fusion.1
  48.5 0.8 broadcast_in_dim.35
  49.3 4.9 %all-to-all-start.2 = ((f32[16,40,128]{2,1,0:T(8,128)}), f32[16,40,128]{2,1,0:T(8,128)S(1)}, u32[]{:S(2)}, u32[]{:S(2)}) async-start(f32[16,40,128]{2,1,0:T(8,128)} %broadcast_in_dim.35), calls=%async_computation.2 | async-start | bytes 655360 | tf_op jit(solution)/shard_map/all_to_all | solution.py:29
  54.2 13.0 %all-to-all-done.2 = f32[16,40,128]{2,1,0:T(8,128)S(1)} async-done(((f32[16,40,128]{2,1,0:T(8,128)}), f32[16,40,128]{2,1,0:T(8,128)S(1)}, u32[]{:S(2)}, u32[]{:S(2)}) %all-to-all-start.2) | async-done | bytes 327712 | tf_op jit(solution)/shard_map/all_to_all | solution.py:29
  67.3 0.4 convolution_bitcast_fusion
  67.8 0.2 fusion.9
  68.0 0.2 fusion.41
  68.4 0.2 fusion.8
  68.6 0.2 fusion.49
  68.8 0.2 fusion.48
  69.0 0.2 fusion.7
  69.1 0.2 fusion.51
  69.3 0.2 fusion.50
  69.5 0.2 fusion.6
  69.6 0.2 fusion.53
  70.0 0.2 fusion.5
  70.1 0.2 fusion.54
  70.3 0.2 fusion.55
  70.5 0.2 fusion.4
  70.6 0.2 convolution_divide_fusion
  70.8 0.4 convolution_convert_fusion.1
  71.3 0.4 convolution_convert_fusion.3
  71.8 0.2 convolution_convert_fusion.4
  72.0 0.2 dot_general.110
  72.3 0.2 convolution_convert_fusion.5
  72.6 10.4 %all_to_all.31 = bf16[16,2,896]{2,1,0:T(2,128)(2,1)S(1)} all-to-all(bf16[16,2,896]{2,1,0:T(2,128)(2,1)S(1)} %copy.56), channel_id=1, replica_groups=mesh['z'=8,'y'=8,'core'=2,'x'=4] {'y','core'}, dimensions={0} | all-to-all | bytes 114688 | tf_op jit(solution)/shard_map/all_to_all | solution.py:105
  83.1 0.7 broadcast_in_dim.36
  83.8 3.9 %all-to-all-start.4 = ((bf16[32,2,896]{2,1,0:T(2,128)(2,1)}), bf16[32,2,896]{2,1,0:T(2,128)(2,1)S(1)}, u32[]{:S(2)}, u32[]{:S(2)}) async-start(bf16[32,2,896]{2,1,0:T(2,128)(2,1)} %broadcast_in_dim.36), calls=%async_computation.4 | async-start | bytes 229376 | tf_op jit(solution)/shard_map/all_to_all | solution.py:29
  87.9 9.5 %all-to-all-done.4 = bf16[32,2,896]{2,1,0:T(2,128)(2,1)S(1)} async-done(((bf16[32,2,896]{2,1,0:T(2,128)(2,1)}), bf16[32,2,896]{2,1,0:T(2,128)(2,1)S(1)}, u32[]{:S(2)}, u32[]{:S(2)}) %all-to-all-start.4) | async-done | bytes 114720 | tf_op jit(solution)/shard_map/all_to_all | solution.py:29
  97.6 0.7 broadcast_in_dim.37
  98.2 4.7 %all-to-all-start.5 = ((bf16[16,2,896]{2,1,0:T(2,128)(2,1)}), bf16[16,2,896]{2,1,0:T(2,128)(2,1)S(1)}, u32[]{:S(2)}, u32[]{:S(2)}) async-start(bf16[16,2,896]{2,1,0:T(2,128)(2,1)} %broadcast_in_dim.37), calls=%async_computation.5 | async-start | bytes 114688 | tf_op jit(solution)/shard_map/all_to_all | solution.py:29
  103.0 0.6 multiply_add_fusion
  103.7 0.2 reshape.108
  103.9 6.8 %all-to-all-done.5 = bf16[16,2,896]{2,1,0:T(2,128)(2,1)S(1)} async-done(((bf16[16,2,896]{2,1,0:T(2,128)(2,1)}), bf16[16,2,896]{2,1,0:T(2,128)(2,1)S(1)}, u32[]{:S(2)}, u32[]{:S(2)}) %all-to-all-start.5) | async-done | bytes 57376 | tf_op jit(solution)/shard_map/all_to_all | solution.py:29
  110.7 0.6 slice_bitcast_fusion.5
  111.3 0.6 slice_bitcast_fusion
  111.9 1.2 %add_convert_fusion.1 = (bf16[288,640]{1,0:T(8,128)(2,1)}, bf16[1,288,640]{2,1,0:T(8,128)(2,1)}) fusion(bf16[288,640]{1,0:T(8,128)(2,1)S(1)} %copy-done.6, bf16[1,288,640]{2,1,0:T(8,128)(2,1)S(1)} %copy-done.3, bf16[1,288,640]{2,1,0:T(8,128)(2,1)S(1)} %copy-done.4, bf16[32,288]{0,1:T(8,128)(2,1)S(1)} %bitcast.103, bf16[32,896]{1,0:T(8,128)(2,1)S(1)} %reshape.107), kind=kOutput, calls=%fused_computation.30 | convolution fusion | flops 13455360 | bytes 1957888 | tf_op jit(solution)/shard_map/rn,rm->nm/dot_general | solution.py:116
  113.1 1.5 %add_convert_fusion = (bf16[1280,256]{1,0:T(8,128)(2,1)}, bf16[1,1280,256]{2,1,0:T(8,128)(2,1)}) fusion(bf16[1280,256]{1,0:T(8,128)(2,1)S(1)} %copy-done.5, bf16[1,1280,256]{2,1,0:T(8,128)(2,1)S(1)} %copy-done.1, bf16[1,1280,256]{2,1,0:T(8,128)(2,1)S(1)} %copy-done.2, bf16[32,1280]{1,0:T(8,128)(2,1)S(1)} %reshape.108, bf16[32,896]{1,0:T(8,128)(2,1)S(1)} %reshape.107), kind=kOutput, calls=%fused_computation.2 | convolution fusion | flops 23920640 | bytes 3375104 | tf_op jit(solution)/shard_map/rn,rm->nm/dot_general | solution.py:116
  (49 shorter events, 2.0 us)
Async XLA Ops:
  0.6 2.1 %copy-start = (bf16[640,32]{0,1:T(8,128)(2,1)S(1)}, bf16[640,32]{0,1:T(8,128)(2,1)}, u32[]{:S(2)}) copy-start(bf16[640,32]{0,1:T(8,128)(2,1)} %param.13) | copy-start | bytes 122884
  1.4 1.8 %copy-start.1 = (bf16[1,1280,256]{2,1,0:T(8,128)(2,1)S(1)}, bf16[1,1280,256]{2,1,0:T(8,128)(2,1)}, u32[]{:S(2)}) copy-start(bf16[1,1280,256]{2,1,0:T(8,128)(2,1)} %param.15) | copy-start | bytes 1966084
  1.4 1.8 %copy-start.2 = (bf16[1,1280,256]{2,1,0:T(8,128)(2,1)S(1)}, bf16[1,1280,256]{2,1,0:T(8,128)(2,1)}, u32[]{:S(2)}) copy-start(bf16[1,1280,256]{2,1,0:T(8,128)(2,1)} %param.14) | copy-start | bytes 1966084
  3.2 0.7 copy-start.7
  23.7 24.3 %all-to-all-start.1 = ((bf16[32,32,128]{2,1,0:T(8,128)(2,1)}), bf16[32,32,128]{2,1,0:T(8,128)(2,1)S(1)}, u32[]{:S(2)}, u32[]{:S(2)}) async-start(bf16[32,32,128]{2,1,0:T(8,128)(2,1)} %broadcast_in_dim.34), calls=%async_computation.1 | async-start | bytes 524288 | tf_op jit(solution)/shard_map/all_to_all | solution.py:29
  49.3 17.9 %all-to-all-start.2 = ((f32[16,40,128]{2,1,0:T(8,128)}), f32[16,40,128]{2,1,0:T(8,128)S(1)}, u32[]{:S(2)}, u32[]{:S(2)}) async-start(f32[16,40,128]{2,1,0:T(8,128)} %broadcast_in_dim.35), calls=%async_computation.2 | async-start | bytes 655360 | tf_op jit(solution)/shard_map/all_to_all | solution.py:29
  72.5 30.5 %copy-start.8 = (f32[64]{0:T(128)S(1)}, f32[64]{0:T(128)}, u32[]{:S(2)}) copy-start(f32[64]{0:T(128)} %param.19) | copy-start | bytes 772
  83.1 28.8 %copy-start.3 = (bf16[1,288,640]{2,1,0:T(8,128)(2,1)S(1)}, bf16[1,288,640]{2,1,0:T(8,128)(2,1)}, u32[]{:S(2)}) copy-start(bf16[1,288,640]{2,1,0:T(8,128)(2,1)} %param.11) | copy-start | bytes 1105924
  83.1 28.8 %copy-start.4 = (bf16[1,288,640]{2,1,0:T(8,128)(2,1)S(1)}, bf16[1,288,640]{2,1,0:T(8,128)(2,1)}, u32[]{:S(2)}) copy-start(bf16[1,288,640]{2,1,0:T(8,128)(2,1)} %param.10) | copy-start | bytes 1105924
  83.1 28.8 %copy-start.6 = (bf16[288,640]{1,0:T(8,128)(2,1)S(1)}, bf16[288,640]{1,0:T(8,128)(2,1)}, u32[]{:S(2)}) copy-start(bf16[288,640]{1,0:T(8,128)(2,1)} %param.12) | copy-start | bytes 1105924
  83.8 13.6 %all-to-all-start.4 = ((bf16[32,2,896]{2,1,0:T(2,128)(2,1)}), bf16[32,2,896]{2,1,0:T(2,128)(2,1)S(1)}, u32[]{:S(2)}, u32[]{:S(2)}) async-start(bf16[32,2,896]{2,1,0:T(2,128)(2,1)} %broadcast_in_dim.36), calls=%async_computation.4 | async-start | bytes 229376 | tf_op jit(solution)/shard_map/all_to_all | solution.py:29
  98.2 12.4 %all-to-all-start.5 = ((bf16[16,2,896]{2,1,0:T(2,128)(2,1)}), bf16[16,2,896]{2,1,0:T(2,128)(2,1)S(1)}, u32[]{:S(2)}, u32[]{:S(2)}) async-start(bf16[16,2,896]{2,1,0:T(2,128)(2,1)} %broadcast_in_dim.37), calls=%async_computation.5 | async-start | bytes 114688 | tf_op jit(solution)/shard_map/all_to_all | solution.py:29
  111.9 1.2 %copy-start.5 = (bf16[1280,256]{1,0:T(8,128)(2,1)S(1)}, bf16[1280,256]{1,0:T(8,128)(2,1)}, u32[]{:S(2)}) copy-start(bf16[1280,256]{1,0:T(8,128)(2,1)} %param.16) | copy-start | bytes 1966084

commit v2 on v1

v2 whole, which is shorter than its diff:
```python
import functools

import jax
import jax.numpy as jnp
from jax import lax
from jax.experimental import pallas as pl
from jax.experimental.pallas import tpu as pltpu
from jax.sharding import Mesh, PartitionSpec as P

NS_ITERS = 6
BETA = 0.9
EPSILON = 1e-06
HIGHEST = lax.Precision.HIGHEST
RANK = 32
LANES = 128
RING = ("y", "core")
CROSS = ("z", "x")
DP = ("z", "y", "core")


def dot(left, right, left_dim, right_dim, precision=None):
    return lax.dot_general(
        left,
        right,
        (((left_dim,), (right_dim,)), ((), ())),
        precision=precision,
        preferred_element_type=jnp.float32,
    )


def inverse_roots(grams):
    row = lax.broadcasted_iota(jnp.int32, (RANK, RANK), 0)
    column = lax.broadcasted_iota(jnp.int32, (RANK, RANK), 1)
    identity = jnp.where(row == column, jnp.float32(1), jnp.float32(0))
    traces = [jnp.sum(g * identity, keepdims=True) + EPSILON for g in grams]
    lefts = [g / t for g, t in zip(grams, traces)]
    middles = [1.5 * identity - 0.5 * y for y in lefts]
    rights = middles
    for repeat_index in range(1, NS_ITERS):
        lefts = [dot(y, m, 1, 0, HIGHEST) for y, m in zip(lefts, middles)]
        middles = [
            1.5 * identity - 0.5 * dot(z, y, 1, 0, HIGHEST) for z, y in zip(rights, lefts)
        ]
        rights = [dot(m, z, 1, 0, HIGHEST) for m, z in zip(middles, rights)]
    return [z / jnp.sqrt(t) for z, t in zip(rights, traces)]


def add(left, right):
    return left.astype(jnp.float32) + right.astype(jnp.float32)


def left_kernel(lg, le, lc, eg, ee, ec, part, lm, em):
    ring = part.shape[0]
    lm[...] = add(lg[0], le[0]).astype(jnp.bfloat16)
    em[...] = add(eg[0], ee[0]).astype(jnp.bfloat16)
    slab = em.shape[0] // ring
    latent_slab = lm.shape[0] // ring
    latent = dot(lc[...], lm[...], 1, 1)
    rest = jnp.zeros((RANK, LANES - slab - latent_slab), jnp.float32)
    for p in range(ring):
        expand = dot(ec[...], em[pl.ds(p * slab, slab), :], 1, 1)
        own = latent[:, p * latent_slab : (p + 1) * latent_slab]
        part[p] = jnp.concatenate([expand, own, rest], axis=1).astype(jnp.bfloat16)


def total(parts):
    whole = parts[0].astype(jnp.float32)
    for p in range(1, parts.shape[0]):
        whole = whole + parts[p].astype(jnp.float32)
    return whole


def sum_kernel(parts, out):
    piece = total(parts).astype(out.dtype)
    for p in range(out.shape[0]):
        out[p] = piece


def gram_kernel(slab, latent_slab, shard, pieces, out):
    depth, shards = pieces.shape[:2]
    half = RANK // 2
    gram = jnp.zeros((RANK, RANK), jnp.float32)
    every = jnp.zeros((RANK, LANES), jnp.float32)
    own = jnp.zeros((RANK, LANES), jnp.float32)
    for x in range(shards):
        piece = total(pieces.at[:, x])
        expand = piece[:, :slab]
        gram = gram + dot(expand, expand, 1, 1, HIGHEST)
        every = every + piece
        own = jnp.where(shard[0] == x, piece, own)
    lower = gram[half:, half:]
    corner = jnp.concatenate([lower[:, : half // 2], lower[:, half // 2 :]], axis=0)
    used = slab + latent_slab
    rest = jnp.zeros((RANK, LANES - used - half - half // 2), jnp.float32)
    mine = jnp.concatenate(
        [own[:, :slab], every[:, slab:used], gram[:, :half], corner, rest], axis=1
    )
    for p in range(out.shape[0]):
        out[p] = mine


def right_kernel(gathered, lm, em, gain, right, lb, eb):
    ring = gathered.shape[0]
    slab = em.shape[0] // ring
    used = slab + lm.shape[0] // ring
    half = RANK // 2
    left = jnp.concatenate([gathered[p, :, slab:used] for p in range(ring)], axis=1)
    latent_gram = dot(left, left, 1, 1, HIGHEST)
    packed = total(gathered)
    first = packed[:, used : used + half]
    corner = packed[:, used + half : used + half + half // 2]
    corner = jnp.concatenate([corner[:half], corner[half:]], axis=1)
    second = jnp.concatenate([first[half:].T, corner], axis=0)
    expand_gram = jnp.concatenate([first, second], axis=1)
    latent_root, expand_root = inverse_roots([latent_gram, expand_gram])
    lb[...] = dot(latent_root, left, 0, 0, HIGHEST).astype(jnp.bfloat16)
    left = jnp.concatenate([gathered[p, :, :slab] for p in range(ring)], axis=1)
    eb[...] = dot(expand_root, left, 0, 0, HIGHEST).astype(jnp.bfloat16)
    tiles = [
        dot(lb[...], lm[...], 1, 0).astype(jnp.bfloat16),
        dot(eb[...], em[...], 1, 0).astype(jnp.bfloat16),
    ]
    p = 0
    for rows in range(0, RANK, half):
        for tile in tiles:
            for at in range(0, tile.shape[1], LANES):
                right[p] = tile[rows : rows + half, at : at + LANES]
                p += 1
    gains = [gain[:, at : at + LANES].astype(jnp.float32) for at in range(0, gain.shape[1], LANES)]
    gains.append(jnp.zeros((half - len(gains), LANES), jnp.float32))
    right[p] = jnp.concatenate(gains, axis=0).astype(jnp.bfloat16)
    for p in range(p + 1, ring):
        right[p] = jnp.zeros(right.shape[1:], right.dtype)


def halves(whole, is_gain):
    high = whole.astype(jnp.bfloat16).astype(jnp.float32)
    low = whole - high
    row = lax.broadcasted_iota(jnp.int32, whole.shape, 0)
    low = jnp.concatenate([low[:2], low[:2], low[4:]], axis=0)
    spare = jnp.logical_and(is_gain, jnp.logical_and(row >= 2, row < 4))
    return jnp.where(spare, low, high).astype(jnp.bfloat16)


def right_sum_kernel(gain_tile, ring, parts, out):
    piece = halves(total(parts), ring[0] == gain_tile)
    for p in range(out.shape[0]):
        out[p] = piece


def factor_kernel(gain_tile, latent_tiles, tiles, replicas, ring, shard, pieces, out):
    depth, shards = pieces.shape[:2]
    is_gain = ring[0] == gain_tile
    crossed = jnp.logical_and(ring[0] < gain_tile, lax.rem(ring[0], tiles) >= latent_tiles)
    whole = jnp.zeros(pieces.shape[2:], jnp.float32)
    for x in range(shards):
        piece = total(pieces.at[:, x])
        whole = whole + jnp.where(jnp.logical_or(crossed, shard[0] == x), piece, 0.0)
    whole = whole / replicas
    joined = jnp.concatenate([whole[:2] + whole[2:4], whole[2:]], axis=0)
    piece = halves(jnp.where(is_gain, joined, whole), is_gain)
    for p in range(out.shape[0]):
        out[p] = piece


def finish_kernel(shard, factors, lb, lg, le, lv, eb, eg, ee, ev, gv, *outs):
    ll, lmom, lf, el, emom, ef, gmom = outs
    half = RANK // 2
    tiles = (lf.shape[1] + ef.shape[1]) // LANES
    first = 0
    for basis, grads, errors, moments, leftover, momentum, out in (
        (lb, lg, le, lv, ll, lmom, lf),
        (eb, eg, ee, ev, el, emom, ef),
    ):
        count = out.shape[1] // LANES
        for t in range(count):
            for upper in range(2):
                out[half * upper : half * (upper + 1), LANES * t : LANES * (t + 1)] = factors[
                    upper * tiles + first + t
                ]
        first += count
        approx = dot(basis[...], out[...], 0, 0)
        leftover[0] = (add(grads[0], errors[0]) - approx).astype(jnp.bfloat16)
        momentum[...] = (BETA * moments[...].astype(jnp.float32) + approx).astype(jnp.bfloat16)
    gain = factors[2 * tiles].astype(jnp.float32)
    gain = gain[:2] + gain[2:4]
    owned = gv.shape[1]
    mean = jnp.zeros((1, owned), jnp.float32)
    for x in range(2 * LANES // owned):
        at = x * owned
        own = gain[at // LANES : at // LANES + 1, at % LANES : at % LANES + owned]
        mean = jnp.where(shard[0] == x, own, mean)
    gmom[...] = BETA * gv[...] + mean


def call(kernel, name, outs, args, scalars=0, fast_in=()):
    specs = [pl.BlockSpec(memory_space=pltpu.SMEM)] * scalars
    specs += [pl.BlockSpec(memory_space=pltpu.VMEM)] * (len(args) - scalars)
    args = [
        pltpu.with_memory_space_constraint(a, pltpu.VMEM) if i in fast_in else a
        for i, a in enumerate(args)
    ]
    shapes = [
        pltpu.VMEM(shape, dtype) if fast else jax.ShapeDtypeStruct(shape, dtype)
        for shape, dtype, fast in outs
    ]
    return pl.pallas_call(
        kernel,
        out_shape=shapes,
        in_specs=specs,
        out_specs=[pl.BlockSpec(memory_space=pltpu.VMEM)] * len(shapes),
        name=name,
    )(*args)


def exchange(array, axes):
    return lax.all_to_all(array, axes, 0, 0)


def local(
    latent_grads,
    latent_errors,
    latent_moments,
    latent_coeffs,
    expand_grads,
    expand_errors,
    expand_moments,
    expand_coeffs,
    gain_grads,
    gain_moments,
):
    ring = lax.axis_size(RING)
    depth = lax.axis_size("z")
    shards = lax.axis_size("x")
    cross = depth * shards
    shard = lax.axis_index("x").astype(jnp.int32).reshape(1)
    place = lax.axis_index(RING).astype(jnp.int32).reshape(1)
    latent_rows, latent_cols = latent_grads.shape[1:]
    expand_rows, expand_cols = expand_grads.shape[1:]
    slab = expand_rows // ring
    latent_slab = latent_rows // ring
    latent_tiles = latent_cols // LANES
    tiles = latent_tiles + expand_cols // LANES
    half = RANK // 2
    bf16, f32 = jnp.bfloat16, jnp.float32

    part, latent_merged, expand_merged = call(
        left_kernel,
        "left",
        (
            ((ring, RANK, LANES), bf16, True),
            ((latent_rows, latent_cols), bf16, True),
            ((expand_rows, expand_cols), bf16, True),
        ),
        (
            latent_grads,
            latent_errors,
            latent_coeffs.T,
            expand_grads,
            expand_errors,
            expand_coeffs.T,
        ),
    )
    part, shard, place = lax.optimization_barrier((part, shard, place))
    part = exchange(part, RING)
    (piece,) = call(sum_kernel, "left_sum", (((cross, RANK, LANES), bf16, True),), (part,), 0, (0,))
    pieces = exchange(piece, CROSS).reshape(depth, shards, RANK, LANES)
    (mine,) = call(
        functools.partial(gram_kernel, slab, latent_slab),
        "gram",
        (((ring, RANK, LANES), f32, True),),
        (shard, pieces),
        1,
        (1,),
    )
    gathered = exchange(mine, RING)
    right, latent_basis, expand_basis = call(
        right_kernel,
        "right",
        (
            ((ring, half, LANES), bf16, True),
            ((RANK, latent_rows), bf16, True),
            ((RANK, expand_rows), bf16, True),
        ),
        (gathered, latent_merged, expand_merged, gain_grads),
        0,
        (0, 1, 2),
    )
    right = exchange(right, RING)
    (piece,) = call(
        functools.partial(right_sum_kernel, 2 * tiles),
        "right_sum",
        (((cross, half, LANES), bf16, True),),
        (place, right),
        1,
        (1,),
    )
    pieces = exchange(piece, CROSS).reshape(depth, shards, half, LANES)
    (mine,) = call(
        functools.partial(factor_kernel, 2 * tiles, latent_tiles, tiles, ring * depth),
        "factor",
        (((ring, half, LANES), bf16, True),),
        (place, shard, pieces),
        2,
        (2,),
    )
    factors = exchange(mine, RING)
    outs = call(
        finish_kernel,
        "finish",
        (
            ((1, latent_rows, latent_cols), bf16, False),
            ((latent_rows, latent_cols), bf16, False),
            ((RANK, latent_cols), bf16, False),
            ((1, expand_rows, expand_cols), bf16, False),
            ((expand_rows, expand_cols), bf16, False),
            ((RANK, expand_cols), bf16, False),
            ((1, gain_moments.shape[0]), f32, False),
        ),
        (
            shard,
            factors,
            latent_basis,
            latent_grads,
            latent_errors,
            latent_moments,
            expand_basis,
            expand_grads,
            expand_errors,
            expand_moments,
            gain_moments.reshape(1, -1),
        ),
        1,
        (1, 2, 6),
    )
    return (*outs[:2], outs[2].T, *outs[3:5], outs[5].T, outs[6].reshape(-1))


def solution(mesh):
    grid = Mesh(mesh.devices.reshape(8, 8, 2, 4), ("z", "y", "core", "x"))
    return jax.shard_map(
        local,
        mesh=grid,
        in_specs=(
            P(DP, None, "x"),
            P(DP, None, "x"),
            P(None, "x"),
            P("x", None),
            P(DP, "x", None),
            P(DP, "x", None),
            P("x", None),
            P(),
            P(DP, None),
            P("x"),
        ),
        out_specs=(
            P(DP, None, "x"),
            P(None, "x"),
            P("x", None),
            P(DP, "x", None),
            P("x", None),
            P(),
            P("x"),
        ),
        check_vma=False,
    )
```

time: 115 us -> 105 us (0.913)
  blocking collectives: 28.9 us -> 93.8 us
  waiting for transfers between devices: 41.6 us -> 0 us
  starting transfers between devices: 25.5 us -> 0 us
  Pallas kernels: 0 us -> 9.63 us
  matrix products: 8.11 us -> 0 us
  local copies, waits for them, and re-layouts: 5.97 us -> 0 us
  other arithmetic: 3.47 us -> 0 us
    all_to_all x2 -> x6, blocking collectives: 28.9 us -> 93.8 us  [exchange(): return lax.all_to_all(array, axes, 0, 0)]
    all_to_all x4 -> x0, waiting for transfers between devices: 41.6 us -> none  [spread(): lax.all_to_all(jnp.broadcast_to(piece, (count, *piece.shape)), axes, 0, 0)]
    all_to_all x4 -> x0, starting transfers between devices: 25.5 us -> none  [spread(): lax.all_to_all(jnp.broadcast_to(piece, (count, *piece.shape)), axes, 0, 0)]
    pallas_call x0 -> x7, Pallas kernels: none -> 9.63 us  [call(): pl.pallas_call(kernel, out_shape=shapes, in_specs=specs, out_specs=[pl.Bl...]
    dot_general x27 -> x0, matrix products: 8.11 us -> none  [the longest x2 2.69 us: finish(): jnp.einsum('rn,rm->nm', basis, factor, preferred_element_type=jnp.float32)]
    broadcast_in_dim x4 -> x0, local copies, waits for them, and re-layouts: 2.86 us -> none  [spread(): jnp.broadcast_to(piece, (count, *piece.shape))]
    convert_element_type x4 -> x0, other arithmetic: 1.48 us -> none  [the longest x1 1.3 us: local(): latent_merged = latent_total.astype(jnp.bfloat16)]
    transpose x2 -> x0, local copies, waits for them, and re-layouts: 1.23 us -> none  [finish(): return (leftover, momentum, factor.T)]
  transfers between devices with their start and end apart: 4 -> 0, of which waited for: 4 -> 0; matrix products, arithmetic and copies ran while one was open for 1% -> 0% of each run, Pallas kernels for 0% -> 0%
where the time goes in v2:
time: 105 us; the launch traced here: 104 us
  blocking collectives  93.8 us (89%)
  Pallas kernels  9.63 us (9%)
    all_to_all x6, blocking collectives, exchange(): return lax.all_to_all(array, axes, 0, 0)  93.8 us
    pallas_call x7, Pallas kernels, call(): pl.pallas_call(kernel, out_shape=shapes, in_specs=specs, out_specs=[pl.Bl...  9.63 us

profile of v2, /device:TPU:1, one launch (start us, length us, event | category | flops | bytes accessed | tf_op | source)
XLA Modules:
  0.0 104.1 jit_solution(6931007774837921158)
XLA Ops:
  0.6 2.0 %left.1 = (bf16[16,32,128]{2,1,0:T(8,128)(2,1)S(1)}, bf16[288,640]{1,0:T(8,128)(2,1)S(1)}, bf16[1280,256]{1,0:T(8,128)(2,1)S(1)}) custom-call(bf16[1,288,640]{2,1,0:T(8,128)(2,1)} %lg.3, bf16[1,288,640]{2,1,0:T(8,128)(2,1)} %le.3, bf16[32,640]{1,0:T(8,128)(2,1)} %bitcast.12, bf16[1,1280,256]{2,1,0:T(8,128)(2,1)} %eg.3, bf16[1,1280,256]{2,1,0:T(8,128)(2,1)} %ee.3, ...), custom_call_target="tpu_custom_call" | custom-call | tf_op jit(solution)/shard_map/left/pallas_call | solution.py:207
  2.6 18.5 %all_to_all.30.parts = bf16[16,32,128]{2,1,0:T(8,128)(2,1)S(1)} all-to-all(bf16[16,32,128]{2,1,0:T(8,128)(2,1)S(1)} %get-tuple-element.26), channel_id=1, replica_groups=mesh['z'=8,'y'=8,'core'=2,'x'=4] {'y','core'}, dimensions={0} | all-to-all | bytes 262144 | tf_op jit(solution)/shard_map/all_to_all | solution.py:217
  21.1 24.1 %all_to_all.31 = bf16[32,32,128]{2,1,0:T(8,128)(2,1)S(1)} all-to-all(bf16[32,32,128]{2,1,0:T(8,128)(2,1)S(1)} %left_sum.1), channel_id=1, replica_groups=mesh['z'=8,'y'=8,'core'=2,'x'=4] {'z','x'}, dimensions={0} | all-to-all | bytes 524288 | tf_op jit(solution)/shard_map/all_to_all | solution.py:217
  45.2 0.4 gram.1
  45.6 15.8 %all_to_all.32.gathered = f32[16,32,128]{2,1,0:T(8,128)S(1)} all-to-all(f32[16,32,128]{2,1,0:T(8,128)S(1)} %gram.1), channel_id=1, replica_groups=mesh['z'=8,'y'=8,'core'=2,'x'=4] {'y','core'}, dimensions={0} | all-to-all | bytes 524288 | tf_op jit(solution)/shard_map/all_to_all | solution.py:217
  61.4 3.6 %right.1 = (bf16[16,16,128]{2,1,0:T(8,128)(2,1)S(1)}, bf16[32,288]{1,0:T(8,128)(2,1)S(1)}, bf16[32,1280]{1,0:T(8,128)(2,1)S(1)}) custom-call(f32[16,32,128]{2,1,0:T(8,128)S(1)} %all_to_all.32.gathered, bf16[288,640]{1,0:T(8,128)(2,1)S(1)} %get-tuple-element.27.lm, bf16[1280,256]{1,0:T(8,128)(2,1)S(1)} %get-tuple-element.28.em, bf16[1,256]{1,0:T(2,128)(2,1)} %gain.1), custom_call_target="tpu_custom_call" | custom-call | tf_op jit(solution)/shard_map/right/pallas_call | solution.py:207
  65.0 10.4 %all_to_all.33.parts = bf16[16,16,128]{2,1,0:T(8,128)(2,1)S(1)} all-to-all(bf16[16,16,128]{2,1,0:T(8,128)(2,1)S(1)} %get-tuple-element.29), channel_id=1, replica_groups=mesh['z'=8,'y'=8,'core'=2,'x'=4] {'y','core'}, dimensions={0} | all-to-all | bytes 131072 | tf_op jit(solution)/shard_map/all_to_all | solution.py:217
  75.5 13.2 %all_to_all.34 = bf16[32,16,128]{2,1,0:T(8,128)(2,1)S(1)} all-to-all(bf16[32,16,128]{2,1,0:T(8,128)(2,1)S(1)} %right_sum.1), channel_id=1, replica_groups=mesh['z'=8,'y'=8,'core'=2,'x'=4] {'z','x'}, dimensions={0} | all-to-all | bytes 262144 | tf_op jit(solution)/shard_map/all_to_all | solution.py:217
  88.7 11.8 %all_to_all.35.factors = bf16[16,16,128]{2,1,0:T(8,128)(2,1)S(1)} all-to-all(bf16[16,16,128]{2,1,0:T(8,128)(2,1)S(1)} %factor.1), channel_id=1, replica_groups=mesh['z'=8,'y'=8,'core'=2,'x'=4] {'y','core'}, dimensions={0} | all-to-all | bytes 131072 | tf_op jit(solution)/shard_map/all_to_all | solution.py:217
  100.5 3.6 %finish.1 = (bf16[1,288,640]{2,1,0:T(8,128)(2,1)}, bf16[288,640]{1,0:T(8,128)(2,1)}, bf16[32,640]{1,0:T(8,128)(2,1)}, bf16[1,1280,256]{2,1,0:T(8,128)(2,1)}, bf1...) custom-call(s32[1]{0:T(128)} %bitcast.2.shard, bf16[16,16,128]{2,1,0:T(8,128)(2,1)S(1)} %all_to_all.35.factors, ...), custom_call_target="tpu_custom_call" | custom-call | tf_op jit(solution)/shard_map/finish/pallas_call | solution.py:207
  (3 shorter events, 0.1 us)

commit v3 on v2

--- a/solution.py
+++ b/solution.py
@@ -13,6 +13,8 @@
 HIGHEST = lax.Precision.HIGHEST
 RANK = 32
 LANES = 128
+EXPAND_CUTS = (0, 256, 512, 768, 1024, 1280)
+LATENT_CUTS = (0, 128, 288)
 RING = ("y", "core")
 CROSS = ("z", "x")
 DP = ("z", "y", "core")
@@ -49,16 +51,32 @@
     return left.astype(jnp.float32) + right.astype(jnp.float32)
 
 
-def left_kernel(lg, le, lc, eg, ee, ec, part, lm, em):
+def left_kernel(lg, le, lc, eg, ee, ec, part, lm, em, lgv, lev, lcv, egv, eev, ecv, sems):
     ring = part.shape[0]
-    lm[...] = add(lg[0], le[0]).astype(jnp.bfloat16)
-    em[...] = add(eg[0], ee[0]).astype(jnp.bfloat16)
     slab = em.shape[0] // ring
     latent_slab = lm.shape[0] // ring
-    latent = dot(lc[...], lm[...], 1, 1)
+    copies = []
+
+    def fetch(source, target):
+        copies.append(pltpu.make_async_copy(source, target, sems.at[len(copies)]))
+        copies[-1].start()
+
+    fetch(lc, lcv)
+    fetch(lg.at[0], lgv)
+    fetch(le.at[0], lev)
+    fetch(ec, ecv)
+    fetch(eg.at[0], egv)
+    fetch(ee.at[0], eev)
+    for c in range(3):
+        copies[c].wait()
+    lm[...] = add(lgv[...], lev[...]).astype(jnp.bfloat16)
+    latent = dot(lcv[...], lm[...], 1, 1)
     rest = jnp.zeros((RANK, LANES - slab - latent_slab), jnp.float32)
+    for copy in copies[3:]:
+        copy.wait()
+    em[...] = add(egv[...], eev[...]).astype(jnp.bfloat16)
     for p in range(ring):
-        expand = dot(ec[...], em[pl.ds(p * slab, slab), :], 1, 1)
+        expand = dot(ecv[...], em[pl.ds(p * slab, slab), :], 1, 1)
         own = latent[:, p * latent_slab : (p + 1) * latent_slab]
         part[p] = jnp.concatenate([expand, own, rest], axis=1).astype(jnp.bfloat16)
 
@@ -163,25 +181,39 @@
         out[p] = piece
 
 
-def finish_kernel(shard, factors, lb, lg, le, lv, eb, eg, ee, ev, gv, *outs):
-    ll, lmom, lf, el, emom, ef, gmom = outs
+def finish_kernel(shard, factors, lb, lg, le, lv, eb, eg, ee, ev, gv, *refs):
+    ll, lmom, lf, el, emom, ef, gmom = refs[:7]
+    llv, lmv, lfv, elv, emv, efv, gmv, sems = refs[7:]
     half = RANK // 2
     tiles = (lf.shape[1] + ef.shape[1]) // LANES
+    copies = []
+
+    def send(source, target):
+        copies.append(pltpu.make_async_copy(source, target, sems.at[len(copies)]))
+        copies[-1].start()
+
     first = 0
-    for basis, grads, errors, moments, leftover, momentum, out in (
-        (lb, lg, le, lv, ll, lmom, lf),
-        (eb, eg, ee, ev, el, emom, ef),
-    ):
-        count = out.shape[1] // LANES
+    for factor, out in ((lfv, lf), (efv, ef)):
+        count = factor.shape[1] // LANES
         for t in range(count):
             for upper in range(2):
-                out[half * upper : half * (upper + 1), LANES * t : LANES * (t + 1)] = factors[
+                factor[half * upper : half * (upper + 1), LANES * t : LANES * (t + 1)] = factors[
                     upper * tiles + first + t
                 ]
         first += count
-        approx = dot(basis[...], out[...], 0, 0)
-        leftover[0] = (add(grads[0], errors[0]) - approx).astype(jnp.bfloat16)
-        momentum[...] = (BETA * moments[...].astype(jnp.float32) + approx).astype(jnp.bfloat16)
+        send(factor, out)
+    for basis, factor, grads, errors, moments, kept, leftover, fresh, momentum, cuts in (
+        (eb, efv, eg, ee, ev, elv, el, emv, emom, EXPAND_CUTS),
+        (lb, lfv, lg, le, lv, llv, ll, lmv, lmom, LATENT_CUTS),
+    ):
+        for low, high in zip(cuts, cuts[1:]):
+            rows = pl.ds(low, high - low)
+            approx = dot(basis[:, low:high], factor[...], 0, 0)
+            whole = add(grads[0, rows, :], errors[0, rows, :])
+            kept[rows, :] = (whole - approx).astype(jnp.bfloat16)
+            send(kept.at[rows], leftover.at[0, rows])
+            fresh[rows, :] = (BETA * moments[rows, :].astype(jnp.float32) + approx).astype(jnp.bfloat16)
+            send(fresh.at[rows], momentum.at[rows])
     gain = factors[2 * tiles].astype(jnp.float32)
     gain = gain[:2] + gain[2:4]
     owned = gv.shape[1]
@@ -190,25 +222,31 @@
         at = x * owned
         own = gain[at // LANES : at // LANES + 1, at % LANES : at % LANES + owned]
         mean = jnp.where(shard[0] == x, own, mean)
-    gmom[...] = BETA * gv[...] + mean
-
-
-def call(kernel, name, outs, args, scalars=0, fast_in=()):
+    gmv[...] = BETA * gv[...] + mean
+    send(gmv, gmom)
+    for copy in copies:
+        copy.wait()
+
+
+def call(kernel, name, outs, args, scalars=0, fast=(), slow=(), scratch=()):
+    args = list(args)
     specs = [pl.BlockSpec(memory_space=pltpu.SMEM)] * scalars
-    specs += [pl.BlockSpec(memory_space=pltpu.VMEM)] * (len(args) - scalars)
-    args = [
-        pltpu.with_memory_space_constraint(a, pltpu.VMEM) if i in fast_in else a
-        for i, a in enumerate(args)
-    ]
+    for i in range(scalars, len(args)):
+        space = pltpu.HBM if i in slow else pltpu.VMEM
+        specs.append(pl.BlockSpec(memory_space=space))
+        if i in slow or i in fast:
+            args[i] = pltpu.with_memory_space_constraint(args[i], space)
     shapes = [
-        pltpu.VMEM(shape, dtype) if fast else jax.ShapeDtypeStruct(shape, dtype)
-        for shape, dtype, fast in outs
+        pltpu.VMEM(shape, dtype) if near else jax.ShapeDtypeStruct(shape, dtype)
+        for shape, dtype, near in outs
     ]
     return pl.pallas_call(
         kernel,
         out_shape=shapes,
         in_specs=specs,
-        out_specs=[pl.BlockSpec(memory_space=pltpu.VMEM)] * len(shapes),
+        out_specs=[pl.BlockSpec(memory_space=pltpu.VMEM if near else pl.ANY) for *_, near in outs],
+        scratch_shapes=scratch,
+        compiler_params=pltpu.CompilerParams(vmem_limit_bytes=16 << 20),
         name=name,
     )(*args)
 
@@ -244,13 +282,14 @@
     half = RANK // 2
     bf16, f32 = jnp.bfloat16, jnp.float32
 
+    latent_shape, expand_shape = (latent_rows, latent_cols), (expand_rows, expand_cols)
     part, latent_merged, expand_merged = call(
         left_kernel,
         "left",
         (
             ((ring, RANK, LANES), bf16, True),
-            ((latent_rows, latent_cols), bf16, True),
-            ((expand_rows, expand_cols), bf16, True),
+            (latent_shape, bf16, True),
+            (expand_shape, bf16, True),
         ),
         (
             latent_grads,
@@ -259,6 +298,16 @@
             expand_grads,
             expand_errors,
             expand_coeffs.T,
+        ),
+        slow=range(6),
+        scratch=(
+            pltpu.VMEM(latent_shape, bf16),
+            pltpu.VMEM(latent_shape, bf16),
+            pltpu.VMEM((RANK, latent_cols), bf16),
+            pltpu.VMEM(expand_shape, bf16),
+            pltpu.VMEM(expand_shape, bf16),
+            pltpu.VMEM((RANK, expand_cols), bf16),
+            pltpu.SemaphoreType.DMA((6,)),
         ),
     )
     part, shard, place = lax.optimization_barrier((part, shard, place))
@@ -305,17 +354,19 @@
         (2,),
     )
     factors = exchange(mine, RING)
+    owned = (1, gain_moments.shape[0])
+    latent_factor, expand_factor = (RANK, latent_cols), (RANK, expand_cols)
     outs = call(
         finish_kernel,
         "finish",
         (
-            ((1, latent_rows, latent_cols), bf16, False),
-            ((latent_rows, latent_cols), bf16, False),
-            ((RANK, latent_cols), bf16, False),
-            ((1, expand_rows, expand_cols), bf16, False),
-            ((expand_rows, expand_cols), bf16, False),
-            ((RANK, expand_cols), bf16, False),
-            ((1, gain_moments.shape[0]), f32, False),
+            ((1, *latent_shape), bf16, False),
+            (latent_shape, bf16, False),
+            (latent_factor, bf16, False),
+            ((1, *expand_shape), bf16, False),
+            (expand_shape, bf16, False),
+            (expand_factor, bf16, False),
+            (owned, f32, False),
         ),
         (
             shard,
@@ -330,8 +381,18 @@
             expand_moments,
             gain_moments.reshape(1, -1),
         ),
-        1,
-        (1, 2, 6),
+        scalars=1,
+        fast=range(1, 11),
+        scratch=(
+            pltpu.VMEM(latent_shape, bf16),
+            pltpu.VMEM(latent_shape, bf16),
+            pltpu.VMEM(latent_factor, bf16),
+            pltpu.VMEM(expand_shape, bf16),
+            pltpu.VMEM(expand_shape, bf16),
+            pltpu.VMEM(expand_factor, bf16),
+            pltpu.VMEM(owned, f32),
+            pltpu.SemaphoreType.DMA((3 + 2 * (len(EXPAND_CUTS) + len(LATENT_CUTS) - 2),)),
+        ),
     )
     return (*outs[:2], outs[2].T, *outs[3:5], outs[5].T, outs[6].reshape(-1))
 

time: 105 us -> 103 us (0.981)
  Pallas kernels: 9.63 us -> 7.13 us
    pallas_call x7, Pallas kernels: 9.63 us -> 7.13 us  [call(): pl.pallas_call(kernel, out_shape=shapes, in_specs=specs, out_specs=[pl.Bl...]
where the time goes in v3:
time: 103 us
  blocking collectives  94.1 us (91%)
  Pallas kernels  7.13 us (7%)
    all_to_all x6, blocking collectives, exchange(): return lax.all_to_all(array, axes, 0, 0)  94.1 us
    pallas_call x7, Pallas kernels, call(): pl.pallas_call(kernel, out_shape=shapes, in_specs=specs, out_specs=[pl.Bl...  7.13 us

profile of v3, /device:TPU:1, one launch (start us, length us, event | category | flops | bytes accessed | tf_op | source)
XLA Modules:
  0.0 102.6 jit_solution(418584662723154396)
XLA Ops:
  0.6 2.0 %left.1 = (bf16[16,32,128]{2,1,0:T(8,128)(2,1)S(1)}, bf16[288,640]{1,0:T(8,128)(2,1)S(1)}, bf16[1280,256]{1,0:T(8,128)(2,1)S(1)}) custom-call(bf16[1,288,640]{2,1,0:T(8,128)(2,1)} %lg.3, bf16[1,288,640]{2,1,0:T(8,128)(2,1)} %le.3, bf16[32,640]{1,0:T(8,128)(2,1)} %bitcast.13, bf16[1,1280,256]{2,1,0:T(8,128)(2,1)} %eg.3, bf16[1,1280,256]{2,1,0:T(8,128)(2,1)} %ee.3, ...), custom_call_target="tpu_custom_call" | custom-call | tf_op jit(solution)/shard_map/left/pallas_call | solution.py:243
  2.6 18.5 %all_to_all.30.parts = bf16[16,32,128]{2,1,0:T(8,128)(2,1)S(1)} all-to-all(bf16[16,32,128]{2,1,0:T(8,128)(2,1)S(1)} %get-tuple-element.26), channel_id=1, replica_groups=mesh['z'=8,'y'=8,'core'=2,'x'=4] {'y','core'}, dimensions={0} | all-to-all | bytes 262144 | tf_op jit(solution)/shard_map/all_to_all | solution.py:255
  21.1 24.1 %all_to_all.31 = bf16[32,32,128]{2,1,0:T(8,128)(2,1)S(1)} all-to-all(bf16[32,32,128]{2,1,0:T(8,128)(2,1)S(1)} %left_sum.1), channel_id=1, replica_groups=mesh['z'=8,'y'=8,'core'=2,'x'=4] {'z','x'}, dimensions={0} | all-to-all | bytes 524288 | tf_op jit(solution)/shard_map/all_to_all | solution.py:255
  45.2 0.0 copy-start.6
  45.2 0.0 copy-start.5
  45.2 0.4 gram.1
  45.6 0.0 copy-start.4
  45.6 16.0 %all_to_all.32.gathered = f32[16,32,128]{2,1,0:T(8,128)S(1)} all-to-all(f32[16,32,128]{2,1,0:T(8,128)S(1)} %gram.1), channel_id=1, replica_groups=mesh['z'=8,'y'=8,'core'=2,'x'=4] {'y','core'}, dimensions={0} | all-to-all | bytes 524288 | tf_op jit(solution)/shard_map/all_to_all | solution.py:255
  61.6 0.0 copy-done.6
  61.6 0.0 copy-start.1
  61.6 0.0 copy-start.2
  61.6 0.0 copy-start.3
  61.6 3.0 %right.1 = (bf16[16,16,128]{2,1,0:T(8,128)(2,1)S(1)}, bf16[32,288]{1,0:T(8,128)(2,1)S(1)}, bf16[32,1280]{1,0:T(8,128)(2,1)S(1)}) custom-call(f32[16,32,128]{2,1,0:T(8,128)S(1)} %all_to_all.32.gathered, bf16[288,640]{1,0:T(8,128)(2,1)S(1)} %get-tuple-element.27.lm, bf16[1280,256]{1,0:T(8,128)(2,1)S(1)} %get-tuple-element.28.em, bf16[1,256]{1,0:T(2,128)(2,1)S(1)} %copy-done.6), custom_call_target="tpu_custom_call" | custom-call | tf_op jit(solution)/shard_map/right/pallas_call | solution.py:243
  64.6 0.0 copy-start
  64.6 10.5 %all_to_all.33.parts = bf16[16,16,128]{2,1,0:T(8,128)(2,1)S(1)} all-to-all(bf16[16,16,128]{2,1,0:T(8,128)(2,1)S(1)} %get-tuple-element.29), channel_id=1, replica_groups=mesh['z'=8,'y'=8,'core'=2,'x'=4] {'y','core'}, dimensions={0} | all-to-all | bytes 131072 | tf_op jit(solution)/shard_map/all_to_all | solution.py:255
  75.1 13.2 %all_to_all.34 = bf16[32,16,128]{2,1,0:T(8,128)(2,1)S(1)} all-to-all(bf16[32,16,128]{2,1,0:T(8,128)(2,1)S(1)} %right_sum.1), channel_id=1, replica_groups=mesh['z'=8,'y'=8,'core'=2,'x'=4] {'z','x'}, dimensions={0} | all-to-all | bytes 262144 | tf_op jit(solution)/shard_map/all_to_all | solution.py:255
  88.4 11.8 %all_to_all.35.factors = bf16[16,16,128]{2,1,0:T(8,128)(2,1)S(1)} all-to-all(bf16[16,16,128]{2,1,0:T(8,128)(2,1)S(1)} %factor.1), channel_id=1, replica_groups=mesh['z'=8,'y'=8,'core'=2,'x'=4] {'y','core'}, dimensions={0} | all-to-all | bytes 131072 | tf_op jit(solution)/shard_map/all_to_all | solution.py:255
  100.2 0.0 copy-start.7
  100.2 0.0 copy-done.5
  100.2 0.0 copy-done.4
  100.2 0.0 copy-done.1
  100.2 0.0 copy-done.2
  100.2 0.0 copy-done.3
  100.2 0.0 copy-done
  100.2 0.6 copy-done.7
  100.8 1.7 %finish.1 = (bf16[1,288,640]{2,1,0:T(8,128)(2,1)}, bf16[288,640]{1,0:T(8,128)(2,1)}, bf16[32,640]{1,0:T(8,128)(2,1)}, bf16[1,1280,256]{2,1,0:T(8,128)(2,1)}, bf1...) custom-call(s32[1]{0:T(128)} %bitcast.2.shard, bf16[16,16,128]{2,1,0:T(8,128)(2,1)S(1)} %all_to_all.35.factors, ...), custom_call_target="tpu_custom_call" | custom-call | tf_op jit(solution)/shard_map/finish/pallas_call | solution.py:243
  (3 shorter events, 0.1 us)
Async XLA Ops:
  45.2 16.4 %copy-start.6 = (bf16[1,256]{1,0:T(2,128)(2,1)S(1)}, bf16[1,256]{1,0:T(2,128)(2,1)}, u32[]{:S(2)}) copy-start(bf16[1,256]{1,0:T(2,128)(2,1)} %gain.1) | copy-start | bytes 1540
  45.2 55.0 %copy-start.5 = (bf16[288,640]{1,0:T(8,128)(2,1)S(1)}, bf16[288,640]{1,0:T(8,128)(2,1)}, u32[]{:S(2)}) copy-start(bf16[288,640]{1,0:T(8,128)(2,1)} %lv.1) | copy-start | bytes 1105924
  45.6 54.6 %copy-start.4 = (bf16[1280,256]{1,0:T(8,128)(2,1)S(1)}, bf16[1280,256]{1,0:T(8,128)(2,1)}, u32[]{:S(2)}) copy-start(bf16[1280,256]{1,0:T(8,128)(2,1)} %ev.1) | copy-start | bytes 1966084
  61.6 38.6 %copy-start.1 = (bf16[1,1280,256]{2,1,0:T(8,128)(2,1)S(1)}, bf16[1,1280,256]{2,1,0:T(8,128)(2,1)}, u32[]{:S(2)}) copy-start(bf16[1,1280,256]{2,1,0:T(8,128)(2,1)} %ee.3) | copy-start | bytes 1966084
  61.6 38.6 %copy-start.2 = (bf16[1,288,640]{2,1,0:T(8,128)(2,1)S(1)}, bf16[1,288,640]{2,1,0:T(8,128)(2,1)}, u32[]{:S(2)}) copy-start(bf16[1,288,640]{2,1,0:T(8,128)(2,1)} %lg.3) | copy-start | bytes 1105924
  61.6 38.6 %copy-start.3 = (bf16[1,288,640]{2,1,0:T(8,128)(2,1)S(1)}, bf16[1,288,640]{2,1,0:T(8,128)(2,1)}, u32[]{:S(2)}) copy-start(bf16[1,288,640]{2,1,0:T(8,128)(2,1)} %le.3) | copy-start | bytes 1105924
  64.6 35.7 %copy-start = (bf16[1,1280,256]{2,1,0:T(8,128)(2,1)S(1)}, bf16[1,1280,256]{2,1,0:T(8,128)(2,1)}, u32[]{:S(2)}) copy-start(bf16[1,1280,256]{2,1,0:T(8,128)(2,1)} %eg.3) | copy-start | bytes 1966084
  100.2 0.7 copy-start.7

commit v4 on v3

--- a/solution.py
+++ b/solution.py
@@ -10,24 +10,29 @@
 NS_ITERS = 6
 BETA = 0.9
 EPSILON = 1e-06
-HIGHEST = lax.Precision.HIGHEST
 RANK = 32
 LANES = 128
 EXPAND_CUTS = (0, 256, 512, 768, 1024, 1280)
 LATENT_CUTS = (0, 128, 288)
-RING = ("y", "core")
-CROSS = ("z", "x")
+RING = ("core", "y")
+CROSS = ("x", "z")
 DP = ("z", "y", "core")
 
 
-def dot(left, right, left_dim, right_dim, precision=None):
-    return lax.dot_general(
-        left,
-        right,
-        (((left_dim,), (right_dim,)), ((), ())),
-        precision=precision,
-        preferred_element_type=jnp.float32,
-    )
+def dot(left, right, left_dim, right_dim):
+    dims = (((left_dim,), (right_dim,)), ((), ()))
+    return lax.dot_general(left, right, dims, preferred_element_type=jnp.float32)
+
+
+def split(whole):
+    high = whole.astype(jnp.bfloat16)
+    return high, (whole - high.astype(jnp.float32)).astype(jnp.bfloat16)
+
+
+def fine_dot(left, right, left_dim, right_dim):
+    (lh, ll), (rh, rl) = split(left), split(right)
+    small = dot(lh, rl, left_dim, right_dim) + dot(ll, rh, left_dim, right_dim)
+    return dot(lh, rh, left_dim, right_dim) + small
 
 
 def inverse_roots(grams):
@@ -39,11 +44,11 @@
     middles = [1.5 * identity - 0.5 * y for y in lefts]
     rights = middles
     for repeat_index in range(1, NS_ITERS):
-        lefts = [dot(y, m, 1, 0, HIGHEST) for y, m in zip(lefts, middles)]
+        lefts = [fine_dot(y, m, 1, 0) for y, m in zip(lefts, middles)]
         middles = [
-            1.5 * identity - 0.5 * dot(z, y, 1, 0, HIGHEST) for z, y in zip(rights, lefts)
+            1.5 * identity - 0.5 * fine_dot(z, y, 1, 0) for z, y in zip(rights, lefts)
         ]
-        rights = [dot(m, z, 1, 0, HIGHEST) for m, z in zip(middles, rights)]
+        rights = [fine_dot(m, z, 1, 0) for m, z in zip(middles, rights)]
     return [z / jnp.sqrt(t) for z, t in zip(rights, traces)]
 
 
@@ -51,7 +56,7 @@
     return left.astype(jnp.float32) + right.astype(jnp.float32)
 
 
-def left_kernel(lg, le, lc, eg, ee, ec, part, lm, em, lgv, lev, lcv, egv, eev, ecv, sems):
+def left_kernel(lg, le, lc, eg, ee, ec, gg, gm, part, lm, em, ggv, gmv, lgv, lev, lcv, egv, eev, ecv, sems):
     ring = part.shape[0]
     slab = em.shape[0] // ring
     latent_slab = lm.shape[0] // ring
@@ -67,6 +72,8 @@
     fetch(ec, ecv)
     fetch(eg.at[0], egv)
     fetch(ee.at[0], eev)
+    fetch(gg, ggv)
+    fetch(gm, gmv)
     for c in range(3):
         copies[c].wait()
     lm[...] = add(lgv[...], lev[...]).astype(jnp.bfloat16)
@@ -95,15 +102,15 @@
 
 
 def gram_kernel(slab, latent_slab, shard, pieces, out):
-    depth, shards = pieces.shape[:2]
+    shards, depth = pieces.shape[:2]
     half = RANK // 2
     gram = jnp.zeros((RANK, RANK), jnp.float32)
     every = jnp.zeros((RANK, LANES), jnp.float32)
     own = jnp.zeros((RANK, LANES), jnp.float32)
     for x in range(shards):
-        piece = total(pieces.at[:, x])
+        piece = total(pieces.at[x])
         expand = piece[:, :slab]
-        gram = gram + dot(expand, expand, 1, 1, HIGHEST)
+        gram = gram + fine_dot(expand, expand, 1, 1)
         every = every + piece
         own = jnp.where(shard[0] == x, piece, own)
     lower = gram[half:, half:]
@@ -118,22 +125,26 @@
 
 
 def right_kernel(gathered, lm, em, gain, right, lb, eb):
-    ring = gathered.shape[0]
+    cores, line = gathered.shape[:2]
+    ring = cores * line
     slab = em.shape[0] // ring
     used = slab + lm.shape[0] // ring
     half = RANK // 2
-    left = jnp.concatenate([gathered[p, :, slab:used] for p in range(ring)], axis=1)
-    latent_gram = dot(left, left, 1, 1, HIGHEST)
-    packed = total(gathered)
+    places = [(p // line, p % line) for p in range(ring)]
+    left = jnp.concatenate([gathered[c, y, :, slab:used] for c, y in places], axis=1)
+    latent_gram = fine_dot(left, left, 1, 1)
+    packed = total(gathered.at[0])
+    for c in range(1, cores):
+        packed = packed + total(gathered.at[c])
     first = packed[:, used : used + half]
     corner = packed[:, used + half : used + half + half // 2]
     corner = jnp.concatenate([corner[:half], corner[half:]], axis=1)
     second = jnp.concatenate([first[half:].T, corner], axis=0)
     expand_gram = jnp.concatenate([first, second], axis=1)
     latent_root, expand_root = inverse_roots([latent_gram, expand_gram])
-    lb[...] = dot(latent_root, left, 0, 0, HIGHEST).astype(jnp.bfloat16)
-    left = jnp.concatenate([gathered[p, :, :slab] for p in range(ring)], axis=1)
-    eb[...] = dot(expand_root, left, 0, 0, HIGHEST).astype(jnp.bfloat16)
+    lb[...] = fine_dot(latent_root, left, 0, 0).astype(jnp.bfloat16)
+    left = jnp.concatenate([gathered[c, y, :, :slab] for c, y in places], axis=1)
+    eb[...] = fine_dot(expand_root, left, 0, 0).astype(jnp.bfloat16)
     tiles = [
         dot(lb[...], lm[...], 1, 0).astype(jnp.bfloat16),
         dot(eb[...], em[...], 1, 0).astype(jnp.bfloat16),
@@ -167,12 +178,12 @@
 
 
 def factor_kernel(gain_tile, latent_tiles, tiles, replicas, ring, shard, pieces, out):
-    depth, shards = pieces.shape[:2]
+    shards, depth = pieces.shape[:2]
     is_gain = ring[0] == gain_tile
     crossed = jnp.logical_and(ring[0] < gain_tile, lax.rem(ring[0], tiles) >= latent_tiles)
     whole = jnp.zeros(pieces.shape[2:], jnp.float32)
     for x in range(shards):
-        piece = total(pieces.at[:, x])
+        piece = total(pieces.at[x])
         whole = whole + jnp.where(jnp.logical_or(crossed, shard[0] == x), piece, 0.0)
     whole = whole / replicas
     joined = jnp.concatenate([whole[:2] + whole[2:4], whole[2:]], axis=0)
@@ -283,13 +294,16 @@
     bf16, f32 = jnp.bfloat16, jnp.float32
 
     latent_shape, expand_shape = (latent_rows, latent_cols), (expand_rows, expand_cols)
-    part, latent_merged, expand_merged = call(
+    owned = (1, gain_moments.shape[0])
+    part, latent_merged, expand_merged, own_gain, gain_before = call(
         left_kernel,
         "left",
         (
             ((ring, RANK, LANES), bf16, True),
             (latent_shape, bf16, True),
             (expand_shape, bf16, True),
+            (gain_grads.shape, bf16, True),
+            (owned, f32, True),
         ),
         (
             latent_grads,
@@ -298,8 +312,10 @@
             expand_grads,
             expand_errors,
             expand_coeffs.T,
-        ),
-        slow=range(6),
+            gain_grads,
+            gain_moments.reshape(owned),
+        ),
+        slow=range(8),
         scratch=(
             pltpu.VMEM(latent_shape, bf16),
             pltpu.VMEM(latent_shape, bf16),
@@ -307,22 +323,22 @@
             pltpu.VMEM(expand_shape, bf16),
             pltpu.VMEM(expand_shape, bf16),
             pltpu.VMEM((RANK, expand_cols), bf16),
-            pltpu.SemaphoreType.DMA((6,)),
+            pltpu.SemaphoreType.DMA((8,)),
         ),
     )
     part, shard, place = lax.optimization_barrier((part, shard, place))
     part = exchange(part, RING)
     (piece,) = call(sum_kernel, "left_sum", (((cross, RANK, LANES), bf16, True),), (part,), 0, (0,))
-    pieces = exchange(piece, CROSS).reshape(depth, shards, RANK, LANES)
+    pieces = exchange(piece, CROSS).reshape(shards, depth, RANK, LANES)
     (mine,) = call(
         functools.partial(gram_kernel, slab, latent_slab),
         "gram",
-        (((ring, RANK, LANES), f32, True),),
+        (((lax.axis_size("y"), RANK, LANES), f32, True),),
         (shard, pieces),
         1,
         (1,),
     )
-    gathered = exchange(mine, RING)
+    gathered = lax.all_gather(exchange(mine, "y"), "core")
     right, latent_basis, expand_basis = call(
         right_kernel,
         "right",
@@ -331,9 +347,9 @@
             ((RANK, latent_rows), bf16, True),
             ((RANK, expand_rows), bf16, True),
         ),
-        (gathered, latent_merged, expand_merged, gain_grads),
+        (gathered, latent_merged, expand_merged, own_gain),
         0,
-        (0, 1, 2),
+        range(4),
     )
     right = exchange(right, RING)
     (piece,) = call(
@@ -344,7 +360,7 @@
         1,
         (1,),
     )
-    pieces = exchange(piece, CROSS).reshape(depth, shards, half, LANES)
+    pieces = exchange(piece, CROSS).reshape(shards, depth, half, LANES)
     (mine,) = call(
         functools.partial(factor_kernel, 2 * tiles, latent_tiles, tiles, ring * depth),
         "factor",
@@ -354,7 +370,6 @@
         (2,),
     )
     factors = exchange(mine, RING)
-    owned = (1, gain_moments.shape[0])
     latent_factor, expand_factor = (RANK, latent_cols), (RANK, expand_cols)
     outs = call(
         finish_kernel,
@@ -379,7 +394,7 @@
             expand_grads,
             expand_errors,
             expand_moments,
-            gain_moments.reshape(1, -1),
+            gain_before,
         ),
         scalars=1,
         fast=range(1, 11),

time: 103 us -> 99.1 us (0.962)
  blocking collectives: 94.1 us -> 91.3 us
    all_to_all x6, blocking collectives: 94.1 us -> 84.6 us  [exchange(): return lax.all_to_all(array, axes, 0, 0)]
    all_gather x0 -> x1, blocking collectives: none -> 6.78 us  [local(): gathered = lax.all_gather(exchange(mine, 'y'), 'core')]
where the time goes in v4:
time: 99.1 us; the launch traced here: 98.7 us
  blocking collectives  91.3 us (92%)
  Pallas kernels  6.65 us (7%)
    all_to_all x6, blocking collectives, exchange(): return lax.all_to_all(array, axes, 0, 0)  84.6 us
    all_gather x1, blocking collectives, local(): gathered = lax.all_gather(exchange(mine, 'y'), 'core')  6.78 us
    pallas_call x7, Pallas kernels, call(): pl.pallas_call(kernel, out_shape=shapes, in_specs=specs, out_specs=[pl.Bl...  6.65 us

profile of v4, /device:TPU:1, one launch (start us, length us, event | category | flops | bytes accessed | tf_op | source)
XLA Modules:
  0.0 98.7 jit_solution(9870552030874416539)
XLA Ops:
  0.6 2.0 %left.1 = (bf16[16,32,128]{2,1,0:T(8,128)(2,1)S(1)}, bf16[288,640]{1,0:T(8,128)(2,1)S(1)}, bf16[1280,256]{1,0:T(8,128)(2,1)S(1)}, bf16[1,256]{1,0:T(2,128)(2,1)S(1)}, f32[1,64]{1,0:T(1,128)S(1)}) custom-call(bf16[1,288,640]{2,1,0:T(8,128)(2,1)} %lg.3, bf16[1,288,640]{2,1,0:T(8,128)(2,1)} %le.3, bf16[32,640]{1,0:T(8,128)(2,1)} %bitcast.14, ...), custom_call_target="tpu_custom_call" | custom-call | tf_op jit(solution)/shard_map/left/pallas_call | solution.py:254
  2.6 16.7 %all_to_all.30.parts = bf16[16,32,128]{2,1,0:T(8,128)(2,1)S(1)} all-to-all(bf16[16,32,128]{2,1,0:T(8,128)(2,1)S(1)} %get-tuple-element.28), channel_id=1, replica_groups=mesh['z'=8,'y'=8,'core'=2,'x'=4] {'core','y'}, dimensions={0} | all-to-all | bytes 262144 | tf_op jit(solution)/shard_map/all_to_all | solution.py:266
  19.4 21.4 %all_to_all.31 = bf16[32,32,128]{2,1,0:T(8,128)(2,1)S(1)} all-to-all(bf16[32,32,128]{2,1,0:T(8,128)(2,1)S(1)} %left_sum.1), channel_id=1, replica_groups=mesh['z'=8,'y'=8,'core'=2,'x'=4] {'x','z'}, dimensions={0} | all-to-all | bytes 524288 | tf_op jit(solution)/shard_map/all_to_all | solution.py:266
  40.7 0.0 copy-start.5
  40.7 0.3 gram.1
  41.0 0.0 copy-start.4
  41.0 11.4 %all_to_all.32 = f32[8,32,128]{2,1,0:T(8,128)S(1)} all-to-all(f32[8,32,128]{2,1,0:T(8,128)S(1)} %gram.1), channel_id=1, replica_groups=mesh['z'=8,'y'=8,'core'=2,'x'=4] {'y'}, dimensions={0} | all-to-all | bytes 262144 | tf_op jit(solution)/shard_map/all_to_all | solution.py:266
  52.5 6.8 %all-gather = f32[16,32,128]{2,1,0:T(8,128)S(1)} all-gather(f32[8,32,128]{2,1,0:T(8,128)S(1)} %all_to_all.32), channel_id=2, replica_groups=mesh['z'=8,'y'=8,'core'=2,'x'=4] {'core'}, dimensions={0}, use_global_device_ids=true | all-gather | bytes 393216 | tf_op jit(solution)/shard_map/all_gather | solution.py:341
  59.3 0.0 copy-start.1
  59.3 0.0 copy-start.2
  59.3 0.0 copy-start.3
  59.3 2.5 %right.1 = (bf16[16,16,128]{2,1,0:T(8,128)(2,1)S(1)}, bf16[32,288]{1,0:T(8,128)(2,1)S(1)}, bf16[32,1280]{1,0:T(8,128)(2,1)S(1)}) custom-call(f32[2,8,32,128]{3,2,1,0:T(8,128)S(1)} %bitcast.12, bf16[288,640]{1,0:T(8,128)(2,1)S(1)} %get-tuple-element.29.lm, bf16[1280,256]{1,0:T(8,128)(2,1)S(1)} %get-tuple-element.30.em, bf16[1,256]{1,0:T(2,128)(2,1)S(1)} %get-tuple-element.31.gain), custom_call_target="tpu_custom_call" | custom-call | tf_op jit(solution)/shard_map/right/pallas_call | solution.py:254
  61.8 0.0 copy-start
  61.8 10.1 %all_to_all.33.parts = bf16[16,16,128]{2,1,0:T(8,128)(2,1)S(1)} all-to-all(bf16[16,16,128]{2,1,0:T(8,128)(2,1)S(1)} %get-tuple-element.32), channel_id=1, replica_groups=mesh['z'=8,'y'=8,'core'=2,'x'=4] {'core','y'}, dimensions={0} | all-to-all | bytes 131072 | tf_op jit(solution)/shard_map/all_to_all | solution.py:266
  72.0 13.1 %all_to_all.34 = bf16[32,16,128]{2,1,0:T(8,128)(2,1)S(1)} all-to-all(bf16[32,16,128]{2,1,0:T(8,128)(2,1)S(1)} %right_sum.1), channel_id=1, replica_groups=mesh['z'=8,'y'=8,'core'=2,'x'=4] {'x','z'}, dimensions={0} | all-to-all | bytes 262144 | tf_op jit(solution)/shard_map/all_to_all | solution.py:266
  85.1 11.9 %all_to_all.35.factors = bf16[16,16,128]{2,1,0:T(8,128)(2,1)S(1)} all-to-all(bf16[16,16,128]{2,1,0:T(8,128)(2,1)S(1)} %factor.1), channel_id=1, replica_groups=mesh['z'=8,'y'=8,'core'=2,'x'=4] {'core','y'}, dimensions={0} | all-to-all | bytes 131072 | tf_op jit(solution)/shard_map/all_to_all | solution.py:266
  97.0 0.0 copy-done.5
  97.0 0.0 copy-done.4
  97.0 0.0 copy-done.1
  97.0 0.0 copy-done.2
  97.0 0.0 copy-done.3
  97.0 0.0 copy-done
  97.0 1.7 %finish.1 = (bf16[1,288,640]{2,1,0:T(8,128)(2,1)}, bf16[288,640]{1,0:T(8,128)(2,1)}, bf16[32,640]{1,0:T(8,128)(2,1)}, bf16[1,1280,256]{2,1,0:T(8,128)(2,1)}, bf1...) custom-call(s32[1]{0:T(128)} %bitcast.3.shard, bf16[16,16,128]{2,1,0:T(8,128)(2,1)S(1)} %all_to_all.35.factors, ...), custom_call_target="tpu_custom_call" | custom-call | tf_op jit(solution)/shard_map/finish/pallas_call | solution.py:254
  (3 shorter events, 0.1 us)
Async XLA Ops:
  40.7 56.2 %copy-start.5 = (bf16[288,640]{1,0:T(8,128)(2,1)S(1)}, bf16[288,640]{1,0:T(8,128)(2,1)}, u32[]{:S(2)}) copy-start(bf16[288,640]{1,0:T(8,128)(2,1)} %lv.1) | copy-start | bytes 1105924
  41.0 55.9 %copy-start.4 = (bf16[1280,256]{1,0:T(8,128)(2,1)S(1)}, bf16[1280,256]{1,0:T(8,128)(2,1)}, u32[]{:S(2)}) copy-start(bf16[1280,256]{1,0:T(8,128)(2,1)} %ev.1) | copy-start | bytes 1966084
  59.3 37.7 %copy-start.1 = (bf16[1,1280,256]{2,1,0:T(8,128)(2,1)S(1)}, bf16[1,1280,256]{2,1,0:T(8,128)(2,1)}, u32[]{:S(2)}) copy-start(bf16[1,1280,256]{2,1,0:T(8,128)(2,1)} %ee.3) | copy-start | bytes 1966084
  59.3 37.7 %copy-start.2 = (bf16[1,288,640]{2,1,0:T(8,128)(2,1)S(1)}, bf16[1,288,640]{2,1,0:T(8,128)(2,1)}, u32[]{:S(2)}) copy-start(bf16[1,288,640]{2,1,0:T(8,128)(2,1)} %lg.3) | copy-start | bytes 1105924
  59.3 37.7 %copy-start.3 = (bf16[1,288,640]{2,1,0:T(8,128)(2,1)S(1)}, bf16[1,288,640]{2,1,0:T(8,128)(2,1)}, u32[]{:S(2)}) copy-start(bf16[1,288,640]{2,1,0:T(8,128)(2,1)} %le.3) | copy-start | bytes 1105924
  61.8 35.2 %copy-start = (bf16[1,1280,256]{2,1,0:T(8,128)(2,1)S(1)}, bf16[1,1280,256]{2,1,0:T(8,128)(2,1)}, u32[]{:S(2)}) copy-start(bf16[1,1280,256]{2,1,0:T(8,128)(2,1)} %eg.3) | copy-start | bytes 1966084

commit v5 on v4

--- a/solution.py
+++ b/solution.py
@@ -12,10 +12,12 @@
 EPSILON = 1e-06
 RANK = 32
 LANES = 128
-EXPAND_CUTS = (0, 256, 512, 768, 1024, 1280)
-LATENT_CUTS = (0, 128, 288)
-RING = ("core", "y")
-CROSS = ("x", "z")
+EXPAND_CUTS = (0, 128, 512, 896, 1280)
+LATENT_CUTS = (0, 288)
+LEFT_OWNERS = ("core", "y")
+LEFT_CROSS = ("x", "z")
+RIGHT_OWNERS = ("core", "z")
+RIGHT_CROSS = ("x", "y")
 DP = ("z", "y", "core")
 
 
@@ -278,12 +280,12 @@
     gain_grads,
     gain_moments,
 ):
-    ring = lax.axis_size(RING)
+    ring = lax.axis_size(LEFT_OWNERS)
     depth = lax.axis_size("z")
     shards = lax.axis_size("x")
     cross = depth * shards
     shard = lax.axis_index("x").astype(jnp.int32).reshape(1)
-    place = lax.axis_index(RING).astype(jnp.int32).reshape(1)
+    place = lax.axis_index(RIGHT_OWNERS).astype(jnp.int32).reshape(1)
     latent_rows, latent_cols = latent_grads.shape[1:]
     expand_rows, expand_cols = expand_grads.shape[1:]
     slab = expand_rows // ring
@@ -327,9 +329,9 @@
         ),
     )
     part, shard, place = lax.optimization_barrier((part, shard, place))
-    part = exchange(part, RING)
+    part = exchange(part, LEFT_OWNERS)
     (piece,) = call(sum_kernel, "left_sum", (((cross, RANK, LANES), bf16, True),), (part,), 0, (0,))
-    pieces = exchange(piece, CROSS).reshape(shards, depth, RANK, LANES)
+    pieces = exchange(piece, LEFT_CROSS).reshape(shards, depth, RANK, LANES)
     (mine,) = call(
         functools.partial(gram_kernel, slab, latent_slab),
         "gram",
@@ -351,7 +353,7 @@
         0,
         range(4),
     )
-    right = exchange(right, RING)
+    right = exchange(right, RIGHT_OWNERS)
     (piece,) = call(
         functools.partial(right_sum_kernel, 2 * tiles),
         "right_sum",
@@ -360,7 +362,7 @@
         1,
         (1,),
     )
-    pieces = exchange(piece, CROSS).reshape(shards, depth, half, LANES)
+    pieces = exchange(piece, RIGHT_CROSS).reshape(shards, depth, half, LANES)
     (mine,) = call(
         functools.partial(factor_kernel, 2 * tiles, latent_tiles, tiles, ring * depth),
         "factor",
@@ -369,7 +371,7 @@
         2,
         (2,),
     )
-    factors = exchange(mine, RING)
+    factors = exchange(mine, RIGHT_OWNERS)
     latent_factor, expand_factor = (RANK, latent_cols), (RANK, expand_cols)
     outs = call(
         finish_kernel,

time: 99.1 us -> 98.5 us (level)
  no operation moved by 1% of the time
where the time goes in v5:
time: 98.5 us; the launch traced here: 98.2 us
  blocking collectives  90.8 us (92%)
  Pallas kernels  6.6 us (7%)
    all_to_all x6, blocking collectives, exchange(): return lax.all_to_all(array, axes, 0, 0)  84 us
    all_gather x1, blocking collectives, local(): gathered = lax.all_gather(exchange(mine, 'y'), 'core')  6.78 us
    pallas_call x7, Pallas kernels, call(): pl.pallas_call(kernel, out_shape=shapes, in_specs=specs, out_specs=[pl.Bl...  6.6 us

profile of v5, /device:TPU:1, one launch (start us, length us, event | category | flops | bytes accessed | tf_op | source)
XLA Modules:
  0.0 98.2 jit_solution(17714800634377971859)
XLA Ops:
  0.6 2.0 %left.1 = (bf16[16,32,128]{2,1,0:T(8,128)(2,1)S(1)}, bf16[288,640]{1,0:T(8,128)(2,1)S(1)}, bf16[1280,256]{1,0:T(8,128)(2,1)S(1)}, bf16[1,256]{1,0:T(2,128)(2,1)S(1)}, f32[1,64]{1,0:T(1,128)S(1)}) custom-call(bf16[1,288,640]{2,1,0:T(8,128)(2,1)} %lg.3, bf16[1,288,640]{2,1,0:T(8,128)(2,1)} %le.3, bf16[32,640]{1,0:T(8,128)(2,1)} %bitcast.14, ...), custom_call_target="tpu_custom_call" | custom-call | tf_op jit(solution)/shard_map/left/pallas_call | solution.py:256
  2.6 16.7 %all_to_all.30.parts = bf16[16,32,128]{2,1,0:T(8,128)(2,1)S(1)} all-to-all(bf16[16,32,128]{2,1,0:T(8,128)(2,1)S(1)} %get-tuple-element.28), channel_id=1, replica_groups=mesh['z'=8,'y'=8,'core'=2,'x'=4] {'core','y'}, dimensions={0} | all-to-all | bytes 262144 | tf_op jit(solution)/shard_map/all_to_all | solution.py:268
  19.4 21.4 %all_to_all.31 = bf16[32,32,128]{2,1,0:T(8,128)(2,1)S(1)} all-to-all(bf16[32,32,128]{2,1,0:T(8,128)(2,1)S(1)} %left_sum.1), channel_id=1, replica_groups=mesh['z'=8,'y'=8,'core'=2,'x'=4] {'x','z'}, dimensions={0} | all-to-all | bytes 524288 | tf_op jit(solution)/shard_map/all_to_all | solution.py:268
  40.7 0.0 copy-start.5
  40.7 0.3 gram.1
  41.0 0.0 copy-start.4
  41.0 11.4 %all_to_all.32 = f32[8,32,128]{2,1,0:T(8,128)S(1)} all-to-all(f32[8,32,128]{2,1,0:T(8,128)S(1)} %gram.1), channel_id=1, replica_groups=mesh['z'=8,'y'=8,'core'=2,'x'=4] {'y'}, dimensions={0} | all-to-all | bytes 262144 | tf_op jit(solution)/shard_map/all_to_all | solution.py:268
  52.5 6.8 %all-gather = f32[16,32,128]{2,1,0:T(8,128)S(1)} all-gather(f32[8,32,128]{2,1,0:T(8,128)S(1)} %all_to_all.32), channel_id=2, replica_groups=mesh['z'=8,'y'=8,'core'=2,'x'=4] {'core'}, dimensions={0}, use_global_device_ids=true | all-gather | bytes 393216 | tf_op jit(solution)/shard_map/all_gather | solution.py:343
  59.3 0.0 copy-start.1
  59.3 0.0 copy-start.2
  59.3 0.0 copy-start.3
  59.3 2.5 %right.1 = (bf16[16,16,128]{2,1,0:T(8,128)(2,1)S(1)}, bf16[32,288]{1,0:T(8,128)(2,1)S(1)}, bf16[32,1280]{1,0:T(8,128)(2,1)S(1)}) custom-call(f32[2,8,32,128]{3,2,1,0:T(8,128)S(1)} %bitcast.12, bf16[288,640]{1,0:T(8,128)(2,1)S(1)} %get-tuple-element.29.lm, bf16[1280,256]{1,0:T(8,128)(2,1)S(1)} %get-tuple-element.30.em, bf16[1,256]{1,0:T(2,128)(2,1)S(1)} %get-tuple-element.31.gain), custom_call_target="tpu_custom_call" | custom-call | tf_op jit(solution)/shard_map/right/pallas_call | solution.py:256
  61.8 0.0 copy-start
  61.8 10.6 %all_to_all.33.parts = bf16[16,16,128]{2,1,0:T(8,128)(2,1)S(1)} all-to-all(bf16[16,16,128]{2,1,0:T(8,128)(2,1)S(1)} %get-tuple-element.32), channel_id=1, replica_groups=mesh['z'=8,'y'=8,'core'=2,'x'=4] {'core','z'}, dimensions={0} | all-to-all | bytes 131072 | tf_op jit(solution)/shard_map/all_to_all | solution.py:268
  72.5 12.2 %all_to_all.34 = bf16[32,16,128]{2,1,0:T(8,128)(2,1)S(1)} all-to-all(bf16[32,16,128]{2,1,0:T(8,128)(2,1)S(1)} %right_sum.1), channel_id=1, replica_groups=mesh['z'=8,'y'=8,'core'=2,'x'=4] {'x','y'}, dimensions={0} | all-to-all | bytes 262144 | tf_op jit(solution)/shard_map/all_to_all | solution.py:268
  84.7 11.7 %all_to_all.35.factors = bf16[16,16,128]{2,1,0:T(8,128)(2,1)S(1)} all-to-all(bf16[16,16,128]{2,1,0:T(8,128)(2,1)S(1)} %factor.1), channel_id=1, replica_groups=mesh['z'=8,'y'=8,'core'=2,'x'=4] {'core','z'}, dimensions={0} | all-to-all | bytes 131072 | tf_op jit(solution)/shard_map/all_to_all | solution.py:268
  96.4 0.0 copy-done.5
  96.4 0.0 copy-done.4
  96.5 0.0 copy-done.1
  96.5 0.0 copy-done.2
  96.5 0.0 copy-done.3
  96.5 0.0 copy-done
  96.5 1.7 %finish.1 = (bf16[1,288,640]{2,1,0:T(8,128)(2,1)}, bf16[288,640]{1,0:T(8,128)(2,1)}, bf16[32,640]{1,0:T(8,128)(2,1)}, bf16[1,1280,256]{2,1,0:T(8,128)(2,1)}, bf1...) custom-call(s32[1]{0:T(128)} %bitcast.3.shard, bf16[16,16,128]{2,1,0:T(8,128)(2,1)S(1)} %all_to_all.35.factors, ...), custom_call_target="tpu_custom_call" | custom-call | tf_op jit(solution)/shard_map/finish/pallas_call | solution.py:256
  (3 shorter events, 0.1 us)
Async XLA Ops:
  40.7 55.7 %copy-start.5 = (bf16[288,640]{1,0:T(8,128)(2,1)S(1)}, bf16[288,640]{1,0:T(8,128)(2,1)}, u32[]{:S(2)}) copy-start(bf16[288,640]{1,0:T(8,128)(2,1)} %lv.1) | copy-start | bytes 1105924
  41.0 55.4 %copy-start.4 = (bf16[1280,256]{1,0:T(8,128)(2,1)S(1)}, bf16[1280,256]{1,0:T(8,128)(2,1)}, u32[]{:S(2)}) copy-start(bf16[1280,256]{1,0:T(8,128)(2,1)} %ev.1) | copy-start | bytes 1966084
  59.3 37.2 %copy-start.1 = (bf16[1,1280,256]{2,1,0:T(8,128)(2,1)S(1)}, bf16[1,1280,256]{2,1,0:T(8,128)(2,1)}, u32[]{:S(2)}) copy-start(bf16[1,1280,256]{2,1,0:T(8,128)(2,1)} %ee.3) | copy-start | bytes 1966084
  59.3 37.2 %copy-start.2 = (bf16[1,288,640]{2,1,0:T(8,128)(2,1)S(1)}, bf16[1,288,640]{2,1,0:T(8,128)(2,1)}, u32[]{:S(2)}) copy-start(bf16[1,288,640]{2,1,0:T(8,128)(2,1)} %lg.3) | copy-start | bytes 1105924
  59.3 37.2 %copy-start.3 = (bf16[1,288,640]{2,1,0:T(8,128)(2,1)S(1)}, bf16[1,288,640]{2,1,0:T(8,128)(2,1)}, u32[]{:S(2)}) copy-start(bf16[1,288,640]{2,1,0:T(8,128)(2,1)} %le.3) | copy-start | bytes 1105924
  61.8 34.7 %copy-start = (bf16[1,1280,256]{2,1,0:T(8,128)(2,1)S(1)}, bf16[1,1280,256]{2,1,0:T(8,128)(2,1)}, u32[]{:S(2)}) copy-start(bf16[1,1280,256]{2,1,0:T(8,128)(2,1)} %eg.3) | copy-start | bytes 1966084

commit v6 on v5

--- a/solution.py
+++ b/solution.py
@@ -81,13 +81,15 @@
     lm[...] = add(lgv[...], lev[...]).astype(jnp.bfloat16)
     latent = dot(lcv[...], lm[...], 1, 1)
     rest = jnp.zeros((RANK, LANES - slab - latent_slab), jnp.float32)
-    for copy in copies[3:]:
+    for copy in copies[3:6]:
         copy.wait()
     em[...] = add(egv[...], eev[...]).astype(jnp.bfloat16)
     for p in range(ring):
         expand = dot(ecv[...], em[pl.ds(p * slab, slab), :], 1, 1)
         own = latent[:, p * latent_slab : (p + 1) * latent_slab]
         part[p] = jnp.concatenate([expand, own, rest], axis=1).astype(jnp.bfloat16)
+    for copy in copies[6:]:
+        copy.wait()
 
 
 def total(parts):

time: 98.5 us -> 98.5 us (level)
  no operation moved by 1% of the time
where the time goes in v6:
time: 98.5 us; the launch traced here: 98.2 us
  blocking collectives  90.8 us (92%)
  Pallas kernels  6.6 us (7%)
    all_to_all x6, blocking collectives, exchange(): return lax.all_to_all(array, axes, 0, 0)  84 us
    all_gather x1, blocking collectives, local(): gathered = lax.all_gather(exchange(mine, 'y'), 'core')  6.78 us
    pallas_call x7, Pallas kernels, call(): pl.pallas_call(kernel, out_shape=shapes, in_specs=specs, out_specs=[pl.Bl...  6.6 us

profile of v6, /device:TPU:1, one launch (start us, length us, event | category | flops | bytes accessed | tf_op | source)
XLA Modules:
  0.0 98.2 jit_solution(6182613687955718542)
XLA Ops:
  0.6 2.0 %left.1 = (bf16[16,32,128]{2,1,0:T(8,128)(2,1)S(1)}, bf16[288,640]{1,0:T(8,128)(2,1)S(1)}, bf16[1280,256]{1,0:T(8,128)(2,1)S(1)}, bf16[1,256]{1,0:T(2,128)(2,1)S(1)}, f32[1,64]{1,0:T(1,128)S(1)}) custom-call(bf16[1,288,640]{2,1,0:T(8,128)(2,1)} %lg.3, bf16[1,288,640]{2,1,0:T(8,128)(2,1)} %le.3, bf16[32,640]{1,0:T(8,128)(2,1)} %bitcast.14, ...), custom_call_target="tpu_custom_call" | custom-call | tf_op jit(solution)/shard_map/left/pallas_call | solution.py:258
  2.6 16.7 %all_to_all.30.parts = bf16[16,32,128]{2,1,0:T(8,128)(2,1)S(1)} all-to-all(bf16[16,32,128]{2,1,0:T(8,128)(2,1)S(1)} %get-tuple-element.28), channel_id=1, replica_groups=mesh['z'=8,'y'=8,'core'=2,'x'=4] {'core','y'}, dimensions={0} | all-to-all | bytes 262144 | tf_op jit(solution)/shard_map/all_to_all | solution.py:270
  19.4 21.4 %all_to_all.31 = bf16[32,32,128]{2,1,0:T(8,128)(2,1)S(1)} all-to-all(bf16[32,32,128]{2,1,0:T(8,128)(2,1)S(1)} %left_sum.1), channel_id=1, replica_groups=mesh['z'=8,'y'=8,'core'=2,'x'=4] {'x','z'}, dimensions={0} | all-to-all | bytes 524288 | tf_op jit(solution)/shard_map/all_to_all | solution.py:270
  40.7 0.0 copy-start.5
  40.7 0.3 gram.1
  41.0 0.0 copy-start.4
  41.0 11.4 %all_to_all.32 = f32[8,32,128]{2,1,0:T(8,128)S(1)} all-to-all(f32[8,32,128]{2,1,0:T(8,128)S(1)} %gram.1), channel_id=1, replica_groups=mesh['z'=8,'y'=8,'core'=2,'x'=4] {'y'}, dimensions={0} | all-to-all | bytes 262144 | tf_op jit(solution)/shard_map/all_to_all | solution.py:270
  52.5 6.8 %all-gather = f32[16,32,128]{2,1,0:T(8,128)S(1)} all-gather(f32[8,32,128]{2,1,0:T(8,128)S(1)} %all_to_all.32), channel_id=2, replica_groups=mesh['z'=8,'y'=8,'core'=2,'x'=4] {'core'}, dimensions={0}, use_global_device_ids=true | all-gather | bytes 393216 | tf_op jit(solution)/shard_map/all_gather | solution.py:345
  59.3 0.0 copy-start.1
  59.3 0.0 copy-start.2
  59.3 0.0 copy-start.3
  59.3 2.5 %right.1 = (bf16[16,16,128]{2,1,0:T(8,128)(2,1)S(1)}, bf16[32,288]{1,0:T(8,128)(2,1)S(1)}, bf16[32,1280]{1,0:T(8,128)(2,1)S(1)}) custom-call(f32[2,8,32,128]{3,2,1,0:T(8,128)S(1)} %bitcast.12, bf16[288,640]{1,0:T(8,128)(2,1)S(1)} %get-tuple-element.29.lm, bf16[1280,256]{1,0:T(8,128)(2,1)S(1)} %get-tuple-element.30.em, bf16[1,256]{1,0:T(2,128)(2,1)S(1)} %get-tuple-element.31.gain), custom_call_target="tpu_custom_call" | custom-call | tf_op jit(solution)/shard_map/right/pallas_call | solution.py:258
  61.8 0.0 copy-start
  61.8 10.6 %all_to_all.33.parts = bf16[16,16,128]{2,1,0:T(8,128)(2,1)S(1)} all-to-all(bf16[16,16,128]{2,1,0:T(8,128)(2,1)S(1)} %get-tuple-element.32), channel_id=1, replica_groups=mesh['z'=8,'y'=8,'core'=2,'x'=4] {'core','z'}, dimensions={0} | all-to-all | bytes 131072 | tf_op jit(solution)/shard_map/all_to_all | solution.py:270
  72.5 12.2 %all_to_all.34 = bf16[32,16,128]{2,1,0:T(8,128)(2,1)S(1)} all-to-all(bf16[32,16,128]{2,1,0:T(8,128)(2,1)S(1)} %right_sum.1), channel_id=1, replica_groups=mesh['z'=8,'y'=8,'core'=2,'x'=4] {'x','y'}, dimensions={0} | all-to-all | bytes 262144 | tf_op jit(solution)/shard_map/all_to_all | solution.py:270
  84.7 11.7 %all_to_all.35.factors = bf16[16,16,128]{2,1,0:T(8,128)(2,1)S(1)} all-to-all(bf16[16,16,128]{2,1,0:T(8,128)(2,1)S(1)} %factor.1), channel_id=1, replica_groups=mesh['z'=8,'y'=8,'core'=2,'x'=4] {'core','z'}, dimensions={0} | all-to-all | bytes 131072 | tf_op jit(solution)/shard_map/all_to_all | solution.py:270
  96.4 0.0 copy-done.5
  96.4 0.0 copy-done.4
  96.5 0.0 copy-done.1
  96.5 0.0 copy-done.2
  96.5 0.0 copy-done.3
  96.5 0.0 copy-done
  96.5 1.7 %finish.1 = (bf16[1,288,640]{2,1,0:T(8,128)(2,1)}, bf16[288,640]{1,0:T(8,128)(2,1)}, bf16[32,640]{1,0:T(8,128)(2,1)}, bf16[1,1280,256]{2,1,0:T(8,128)(2,1)}, bf1...) custom-call(s32[1]{0:T(128)} %bitcast.3.shard, bf16[16,16,128]{2,1,0:T(8,128)(2,1)S(1)} %all_to_all.35.factors, ...), custom_call_target="tpu_custom_call" | custom-call | tf_op jit(solution)/shard_map/finish/pallas_call | solution.py:258
  (3 shorter events, 0.1 us)
Async XLA Ops:
  40.7 55.7 %copy-start.5 = (bf16[288,640]{1,0:T(8,128)(2,1)S(1)}, bf16[288,640]{1,0:T(8,128)(2,1)}, u32[]{:S(2)}) copy-start(bf16[288,640]{1,0:T(8,128)(2,1)} %lv.1) | copy-start | bytes 1105924
  41.0 55.4 %copy-start.4 = (bf16[1280,256]{1,0:T(8,128)(2,1)S(1)}, bf16[1280,256]{1,0:T(8,128)(2,1)}, u32[]{:S(2)}) copy-start(bf16[1280,256]{1,0:T(8,128)(2,1)} %ev.1) | copy-start | bytes 1966084
  59.3 37.2 %copy-start.1 = (bf16[1,1280,256]{2,1,0:T(8,128)(2,1)S(1)}, bf16[1,1280,256]{2,1,0:T(8,128)(2,1)}, u32[]{:S(2)}) copy-start(bf16[1,1280,256]{2,1,0:T(8,128)(2,1)} %ee.3) | copy-start | bytes 1966084
  59.3 37.2 %copy-start.2 = (bf16[1,288,640]{2,1,0:T(8,128)(2,1)S(1)}, bf16[1,288,640]{2,1,0:T(8,128)(2,1)}, u32[]{:S(2)}) copy-start(bf16[1,288,640]{2,1,0:T(8,128)(2,1)} %lg.3) | copy-start | bytes 1105924
  59.3 37.2 %copy-start.3 = (bf16[1,288,640]{2,1,0:T(8,128)(2,1)S(1)}, bf16[1,288,640]{2,1,0:T(8,128)(2,1)}, u32[]{:S(2)}) copy-start(bf16[1,288,640]{2,1,0:T(8,128)(2,1)} %le.3) | copy-start | bytes 1105924
  61.8 34.7 %copy-start = (bf16[1,1280,256]{2,1,0:T(8,128)(2,1)S(1)}, bf16[1,1280,256]{2,1,0:T(8,128)(2,1)}, u32[]{:S(2)}) copy-start(bf16[1,1280,256]{2,1,0:T(8,128)(2,1)} %eg.3) | copy-start | bytes 1966084

commit v7 on v5

--- a/solution.py
+++ b/solution.py
@@ -15,7 +15,7 @@
 EXPAND_CUTS = (0, 128, 512, 896, 1280)
 LATENT_CUTS = (0, 288)
 LEFT_OWNERS = ("core", "y")
-LEFT_CROSS = ("x", "z")
+LEFT_CROSS = ("z", "x")
 RIGHT_OWNERS = ("core", "z")
 RIGHT_CROSS = ("x", "y")
 DP = ("z", "y", "core")
@@ -104,13 +104,13 @@
 
 
 def gram_kernel(slab, latent_slab, shard, pieces, out):
-    shards, depth = pieces.shape[:2]
+    depth, shards = pieces.shape[:2]
     half = RANK // 2
     gram = jnp.zeros((RANK, RANK), jnp.float32)
     every = jnp.zeros((RANK, LANES), jnp.float32)
     own = jnp.zeros((RANK, LANES), jnp.float32)
     for x in range(shards):
-        piece = total(pieces.at[x])
+        piece = total(pieces.at[:, x])
         expand = piece[:, :slab]
         gram = gram + fine_dot(expand, expand, 1, 1)
         every = every + piece
@@ -331,7 +331,7 @@
     part, shard, place = lax.optimization_barrier((part, shard, place))
     part = exchange(part, LEFT_OWNERS)
     (piece,) = call(sum_kernel, "left_sum", (((cross, RANK, LANES), bf16, True),), (part,), 0, (0,))
-    pieces = exchange(piece, LEFT_CROSS).reshape(shards, depth, RANK, LANES)
+    pieces = exchange(piece, LEFT_CROSS).reshape(depth, shards, RANK, LANES)
     (mine,) = call(
         functools.partial(gram_kernel, slab, latent_slab),
         "gram",

time: 98.5 us -> 98.5 us (level)
    all_gather x1, blocking collectives: 6.78 us -> 5.36 us  [local(): gathered = lax.all_gather(exchange(mine, 'y'), 'core')]
    all_to_all x6, blocking collectives: 84 us -> 85.4 us  [exchange(): return lax.all_to_all(array, axes, 0, 0)]
where the time goes in v7:
time: 98.5 us; the launch traced here: 98.1 us
  blocking collectives  90.7 us (92%)
  Pallas kernels  6.6 us (7%)
    all_to_all x6, blocking collectives, exchange(): return lax.all_to_all(array, axes, 0, 0)  85.4 us
    pallas_call x7, Pallas kernels, call(): pl.pallas_call(kernel, out_shape=shapes, in_specs=specs, out_specs=[pl.Bl...  6.6 us
    all_gather x1, blocking collectives, local(): gathered = lax.all_gather(exchange(mine, 'y'), 'core')  5.36 us

profile of v7, /device:TPU:1, one launch (start us, length us, event | category | flops | bytes accessed | tf_op | source)
XLA Modules:
  0.0 98.1 jit_solution(6273040936721639778)
XLA Ops:
  0.6 2.0 %left.1 = (bf16[16,32,128]{2,1,0:T(8,128)(2,1)S(1)}, bf16[288,640]{1,0:T(8,128)(2,1)S(1)}, bf16[1280,256]{1,0:T(8,128)(2,1)S(1)}, bf16[1,256]{1,0:T(2,128)(2,1)S(1)}, f32[1,64]{1,0:T(1,128)S(1)}) custom-call(bf16[1,288,640]{2,1,0:T(8,128)(2,1)} %lg.3, bf16[1,288,640]{2,1,0:T(8,128)(2,1)} %le.3, bf16[32,640]{1,0:T(8,128)(2,1)} %bitcast.14, ...), custom_call_target="tpu_custom_call" | custom-call | tf_op jit(solution)/shard_map/left/pallas_call | solution.py:256
  2.6 16.7 %all_to_all.30.parts = bf16[16,32,128]{2,1,0:T(8,128)(2,1)S(1)} all-to-all(bf16[16,32,128]{2,1,0:T(8,128)(2,1)S(1)} %get-tuple-element.28), channel_id=1, replica_groups=mesh['z'=8,'y'=8,'core'=2,'x'=4] {'core','y'}, dimensions={0} | all-to-all | bytes 262144 | tf_op jit(solution)/shard_map/all_to_all | solution.py:268
  19.4 22.3 %all_to_all.31 = bf16[32,32,128]{2,1,0:T(8,128)(2,1)S(1)} all-to-all(bf16[32,32,128]{2,1,0:T(8,128)(2,1)S(1)} %left_sum.1), channel_id=1, replica_groups=mesh['z'=8,'y'=8,'core'=2,'x'=4] {'z','x'}, dimensions={0} | all-to-all | bytes 524288 | tf_op jit(solution)/shard_map/all_to_all | solution.py:268
  41.7 0.0 copy-start.5
  41.7 0.3 gram.1
  42.0 0.0 copy-start.4
  42.0 12.3 %all_to_all.32 = f32[8,32,128]{2,1,0:T(8,128)S(1)} all-to-all(f32[8,32,128]{2,1,0:T(8,128)S(1)} %gram.1), channel_id=1, replica_groups=mesh['z'=8,'y'=8,'core'=2,'x'=4] {'y'}, dimensions={0} | all-to-all | bytes 262144 | tf_op jit(solution)/shard_map/all_to_all | solution.py:268
  54.3 5.4 %all-gather = f32[16,32,128]{2,1,0:T(8,128)S(1)} all-gather(f32[8,32,128]{2,1,0:T(8,128)S(1)} %all_to_all.32), channel_id=2, replica_groups=mesh['z'=8,'y'=8,'core'=2,'x'=4] {'core'}, dimensions={0}, use_global_device_ids=true | all-gather | bytes 393216 | tf_op jit(solution)/shard_map/all_gather | solution.py:343
  59.6 0.0 copy-start.1
  59.6 0.0 copy-start.2
  59.6 0.0 copy-start.3
  59.6 2.5 %right.1 = (bf16[16,16,128]{2,1,0:T(8,128)(2,1)S(1)}, bf16[32,288]{1,0:T(8,128)(2,1)S(1)}, bf16[32,1280]{1,0:T(8,128)(2,1)S(1)}) custom-call(f32[2,8,32,128]{3,2,1,0:T(8,128)S(1)} %bitcast.12, bf16[288,640]{1,0:T(8,128)(2,1)S(1)} %get-tuple-element.29.lm, bf16[1280,256]{1,0:T(8,128)(2,1)S(1)} %get-tuple-element.30.em, bf16[1,256]{1,0:T(2,128)(2,1)S(1)} %get-tuple-element.31.gain), custom_call_target="tpu_custom_call" | custom-call | tf_op jit(solution)/shard_map/right/pallas_call | solution.py:256
  62.2 0.0 copy-start
  62.2 10.2 %all_to_all.33.parts = bf16[16,16,128]{2,1,0:T(8,128)(2,1)S(1)} all-to-all(bf16[16,16,128]{2,1,0:T(8,128)(2,1)S(1)} %get-tuple-element.32), channel_id=1, replica_groups=mesh['z'=8,'y'=8,'core'=2,'x'=4] {'core','z'}, dimensions={0} | all-to-all | bytes 131072 | tf_op jit(solution)/shard_map/all_to_all | solution.py:268
  72.4 12.1 %all_to_all.34 = bf16[32,16,128]{2,1,0:T(8,128)(2,1)S(1)} all-to-all(bf16[32,16,128]{2,1,0:T(8,128)(2,1)S(1)} %right_sum.1), channel_id=1, replica_groups=mesh['z'=8,'y'=8,'core'=2,'x'=4] {'x','y'}, dimensions={0} | all-to-all | bytes 262144 | tf_op jit(solution)/shard_map/all_to_all | solution.py:268
  84.6 11.8 %all_to_all.35.factors = bf16[16,16,128]{2,1,0:T(8,128)(2,1)S(1)} all-to-all(bf16[16,16,128]{2,1,0:T(8,128)(2,1)S(1)} %factor.1), channel_id=1, replica_groups=mesh['z'=8,'y'=8,'core'=2,'x'=4] {'core','z'}, dimensions={0} | all-to-all | bytes 131072 | tf_op jit(solution)/shard_map/all_to_all | solution.py:268
  96.4 0.0 copy-done.5
  96.4 0.0 copy-done.4
  96.4 0.0 copy-done.1
  96.4 0.0 copy-done.2
  96.4 0.0 copy-done.3
  96.4 0.0 copy-done
  96.4 1.7 %finish.1 = (bf16[1,288,640]{2,1,0:T(8,128)(2,1)}, bf16[288,640]{1,0:T(8,128)(2,1)}, bf16[32,640]{1,0:T(8,128)(2,1)}, bf16[1,1280,256]{2,1,0:T(8,128)(2,1)}, bf1...) custom-call(s32[1]{0:T(128)} %bitcast.3.shard, bf16[16,16,128]{2,1,0:T(8,128)(2,1)S(1)} %all_to_all.35.factors, ...), custom_call_target="tpu_custom_call" | custom-call | tf_op jit(solution)/shard_map/finish/pallas_call | solution.py:256
  (3 shorter events, 0.1 us)
Async XLA Ops:
  41.7 54.7 %copy-start.5 = (bf16[288,640]{1,0:T(8,128)(2,1)S(1)}, bf16[288,640]{1,0:T(8,128)(2,1)}, u32[]{:S(2)}) copy-start(bf16[288,640]{1,0:T(8,128)(2,1)} %lv.1) | copy-start | bytes 1105924
  42.0 54.4 %copy-start.4 = (bf16[1280,256]{1,0:T(8,128)(2,1)S(1)}, bf16[1280,256]{1,0:T(8,128)(2,1)}, u32[]{:S(2)}) copy-start(bf16[1280,256]{1,0:T(8,128)(2,1)} %ev.1) | copy-start | bytes 1966084
  59.6 36.7 %copy-start.1 = (bf16[1,1280,256]{2,1,0:T(8,128)(2,1)S(1)}, bf16[1,1280,256]{2,1,0:T(8,128)(2,1)}, u32[]{:S(2)}) copy-start(bf16[1,1280,256]{2,1,0:T(8,128)(2,1)} %ee.3) | copy-start | bytes 1966084
  59.6 36.7 %copy-start.2 = (bf16[1,288,640]{2,1,0:T(8,128)(2,1)S(1)}, bf16[1,288,640]{2,1,0:T(8,128)(2,1)}, u32[]{:S(2)}) copy-start(bf16[1,288,640]{2,1,0:T(8,128)(2,1)} %lg.3) | copy-start | bytes 1105924
  59.6 36.7 %copy-start.3 = (bf16[1,288,640]{2,1,0:T(8,128)(2,1)S(1)}, bf16[1,288,640]{2,1,0:T(8,128)(2,1)}, u32[]{:S(2)}) copy-start(bf16[1,288,640]{2,1,0:T(8,128)(2,1)} %le.3) | copy-start | bytes 1105924
  62.2 34.2 %copy-start = (bf16[1,1280,256]{2,1,0:T(8,128)(2,1)S(1)}, bf16[1,1280,256]{2,1,0:T(8,128)(2,1)}, u32[]{:S(2)}) copy-start(bf16[1,1280,256]{2,1,0:T(8,128)(2,1)} %eg.3) | copy-start | bytes 1966084
